TPU v7x, 32 devices: a whole 2x2x4 slice. The times are simulated.
32 devices in a mesh: expert: 8 (over z, y), tensor: 4 (over x, core).
Axes of the slice: x: 2, y: 2, z: 4, core: 2. Of those that a mesh axis runs over, the one named last changes fastest.
Arguments:
- inputs: bfloat16 [12608, 512], P('expert'), may hold values from -6 to 6
- gain_attend: float32 [512], replicated, may hold values from 0.25 to 1.75
- triple_weight: bfloat16 [512, 3, 512], P(None, None, 'tensor'), may hold values from -0.25 to 0.25
- project_weight: bfloat16 [512, 512], P('tensor'), may hold values from -1.5 to 1.5
- gain_mixture: float32 [512], replicated, may hold values from 0.25 to 1.75
- router_weight: bfloat16 [512, 16], replicated, may hold values from -0.125 to 0.125
- expert_first: bfloat16 [16, 512, 2048], P('expert', None, 'tensor'), may hold values from -0.25 to 0.25
- expert_second: bfloat16 [16, 2048, 512], P('expert', 'tensor'), may hold values from -0.1875 to 0.1875
- triple_down: bfloat16 [512, 128], replicated, may hold values from -0.25 to 0.25
- triple_up: bfloat16 [128, 3, 512], P(None, None, 'tensor'), may hold values from -1.5 to 1.5
- project_down: bfloat16 [512, 128], P('tensor'), may hold values from -1.5 to 1.5
- project_up: bfloat16 [128, 512], replicated, may hold values from -1.5 to 1.5
- router_down: bfloat16 [512, 128], replicated, may hold values from -0.25 to 0.25
- router_up: bfloat16 [128, 16], replicated, may hold values from -0.75 to 0.75
- first_down: bfloat16 [512, 128], replicated, may hold values from -0.25 to 0.25
- first_up: bfloat16 [128, 2048], P(None, 'tensor'), may hold values from -1.5 to 1.5
- second_down: bfloat16 [2048, 128], P('tensor'), may hold values from -0.1875 to 0.1875
- second_up: bfloat16 [128, 512], replicated, may hold values from -1.5 to 1.5
- adapter_index: int32 [64], P('expert'), may hold values from 0 to 7
- routes: int32 [12608, 2], P('expert'), may hold values from 0 to 15, all different within a row
- priority: int32 [8, 1576], P('expert'), may hold values from 0 to 1575, each once within a row
- cotangent: bfloat16 [12608, 512], P('expert'), may hold values from -6 to 6
Outputs:
- block_output: bfloat16 [12608, 512], P('expert')
- input_grad: bfloat16 [12608, 512], P('expert')
- triple_down_grad: float32 [512, 128], replicated
- triple_up_grad: float32 [128, 3, 512], P(None, None, 'tensor')
- project_down_grad: float32 [512, 128], P('tensor')
- project_up_grad: float32 [128, 512], replicated
- router_down_grad: float32 [512, 128], replicated
- router_up_grad: float32 [128, 16], replicated
- first_down_grad: float32 [512, 128], replicated
- first_up_grad: float32 [128, 2048], P(None, 'tensor')
- second_down_grad: float32 [2048, 128], P('tensor')
- second_up_grad: float32 [128, 512], replicated
Inputs may be any that keep to these rules, and one draw needn't show every extreme that they name: `routes`: each row names 2 different experts. `priority`: each row holds every token index of its group once.
All inputs are finite; a program needn't handle non-finite values.
Results may differ from a plain program's by a relative error of at most 0.028.
Values may be sent and summed in bfloat16 or wider, within the bound.
A program may use at most 192 MiB of HBM per device.

v0:
```python
import jax
import jax.numpy as jnp
from jax import lax
from jax.sharding import PartitionSpec as P

HEAD_DIM = 64
TOP = 2
ADAPTERS = 8
RANK = 16


highest = lax.Precision.HIGHEST
norm_eps = 1e-06


def norm_rows(values, gain):
    centre = jnp.mean(values, axis=-1, keepdims=True)
    shifted = values - centre
    spread = jnp.mean(shifted * shifted, axis=-1, keepdims=True)
    return shifted * lax.rsqrt(spread + norm_eps) * gain


def pick_columns(token_ids):
    column = jnp.arange(ADAPTERS * RANK, dtype=jnp.int32) // RANK
    return (token_ids[:, None] == column[None, :]).astype(jnp.float32)


def place_pairs(route_rows, ranking, capacity, experts):
    count = ranking.shape[0]
    ranked = route_rows[ranking]
    pair_expert = jnp.concatenate([ranked[:, 0], ranked[:, 1]])
    pair_token = jnp.concatenate([ranking, ranking])
    onehot = (pair_expert[:, None] == jnp.arange(experts, dtype=jnp.int32)[None, :]).astype(
        jnp.int32
    )
    position = jnp.sum(jnp.cumsum(onehot, axis=0) * onehot, axis=1) - 1
    kept_pair = position < capacity
    pair_slot = pair_expert * capacity + jnp.minimum(position, capacity - 1)
    target = jnp.where(kept_pair, pair_slot, experts * capacity)
    slot_token = (
        jnp.full((experts * capacity,), count, jnp.int32).at[target].set(pair_token, mode="drop")
    )
    slot_first = jnp.zeros((count,), jnp.int32).at[ranking].set(pair_slot[:count])
    slot_second = jnp.zeros((count,), jnp.int32).at[ranking].set(pair_slot[count:])
    keep_first = jnp.zeros((count,), jnp.int32).at[ranking].set(kept_pair[:count].astype(jnp.int32))
    keep_second = (
        jnp.zeros((count,), jnp.int32).at[ranking].set(kept_pair[count:].astype(jnp.int32))
    )
    return (
        slot_token,
        jnp.stack([slot_first, slot_second], axis=1),
        jnp.stack([keep_first, keep_second], axis=1),
    )


def to_experts(row_block, slot_ids):
    row_block, slot_ids = (
        lax.all_to_all(row_block, "expert", split_axis=0, concat_axis=0, tiled=True),
        lax.all_to_all(slot_ids, "expert", split_axis=0, concat_axis=0, tiled=True),
    )
    return (row_block, slot_ids)


def from_experts(partial_value):
    summed = lax.psum(partial_value.astype(jnp.bfloat16), "tensor")
    row_block = lax.all_to_all(summed, "expert", split_axis=0, concat_axis=0, tiled=True)
    return row_block


def body(
    inputs,
    gain_attend,
    triple_weight,
    project_weight,
    gain_mixture,
    router_weight,
    expert_first,
    expert_second,
    triple_down,
    triple_up,
    project_down,
    project_up,
    router_down,
    router_up,
    first_down,
    first_up,
    second_down,
    second_up,
    adapter_index,
    routes,
    priority,
    cotangent,
):
    f32 = jnp.float32
    bf16 = jnp.bfloat16
    tok_count, model_width = inputs.shape
    images = adapter_index.shape[0]
    seq_len = tok_count // images
    local_heads = triple_weight.shape[2] // HEAD_DIM
    local_width = triple_weight.shape[2]
    tensor_count = lax.axis_size("tensor")
    local_experts = expert_first.shape[0]
    experts = router_weight.shape[1]
    capacity = tensor_count * (
        (5 * tok_count * TOP + 4 * tensor_count * experts - 1) // (4 * tensor_count * experts)
    )
    score_scale = HEAD_DIM ** (-0.5)
    adapt_width = ADAPTERS * RANK
    token_ids = jnp.repeat(adapter_index, seq_len, total_repeat_length=tok_count)
    pick_cols = pick_columns(token_ids)
    source = inputs.astype(f32)
    normed1, norm1_back = jax.vjp(lambda values: norm_rows(values, gain_attend), source)
    attn_in = normed1.astype(bf16)
    triple_flat = triple_weight.reshape(model_width, 3 * local_width)
    triple_high = triple_up.reshape(adapt_width, 3 * local_width)
    triple_low = (jnp.dot(attn_in, triple_down, preferred_element_type=f32) * pick_cols).astype(
        bf16
    )
    triple = jnp.dot(attn_in, triple_flat, preferred_element_type=f32) + jnp.dot(
        triple_low, triple_high, preferred_element_type=f32
    )
    triple = triple.astype(bf16).reshape(images, seq_len, 3, local_heads, HEAD_DIM)
    queries = triple[:, :, 0]
    key_rows = triple[:, :, 1]
    value_rows = triple[:, :, 2]
    scores = (
        jnp.einsum("bqhd,bkhd->bhqk", queries, key_rows, preferred_element_type=f32) * score_scale
    )
    row_max = jnp.max(scores, axis=-1, keepdims=True)
    shifted = jnp.exp(scores - row_max)
    row_total = jnp.sum(shifted, axis=-1, keepdims=True)
    log_total = row_max + jnp.log(row_total)
    probs = (shifted / row_total).astype(bf16)
    attended = (
        jnp.einsum("bhqk,bkhd->bqhd", probs, value_rows, preferred_element_type=f32)
        .reshape(tok_count, local_width)
        .astype(bf16)
    )
    branch_part = jnp.dot(attended, project_weight, preferred_element_type=f32)
    project_part = jnp.dot(attended, project_down, preferred_element_type=f32)
    branch_sum, project_sum = (
        lax.psum(branch_part.astype(jnp.bfloat16), "tensor").astype(jnp.float32),
        lax.psum(project_part.astype(jnp.bfloat16), "tensor").astype(jnp.float32),
    )
    project_low = (project_sum * pick_cols).astype(bf16)
    middle = source + branch_sum + jnp.dot(project_low, project_up, preferred_element_type=f32)
    normed2, norm2_back = jax.vjp(lambda values: norm_rows(values, gain_mixture), middle)
    mixed_in = normed2.astype(bf16)
    router_low = jnp.dot(mixed_in, router_down, preferred_element_type=f32) * pick_cols
    logits = jnp.dot(mixed_in, router_weight, preferred_element_type=f32) + jnp.dot(
        router_low, router_up.astype(f32), precision=highest
    )
    chosen = (routes[:, :, None] == jnp.arange(experts, dtype=jnp.int32)[None, None, :]).astype(f32)
    picked = jnp.sum(chosen * logits[:, None, :], axis=-1)
    gate_prob = jax.nn.softmax(picked, axis=-1)
    slot_token, slot_pairs, keep_pairs = place_pairs(routes, priority[0], capacity, experts)
    keep_float = keep_pairs.astype(f32)
    gate_wts = gate_prob * keep_float
    padded = jnp.concatenate([mixed_in, jnp.zeros((1, model_width), bf16)], axis=0)
    send_rows = padded[slot_token].reshape(experts, capacity, model_width)
    id_pad = jnp.concatenate([token_ids, jnp.zeros((1,), jnp.int32)])
    send_ids = id_pad[slot_token].reshape(experts, capacity)
    got_rows, got_ids = to_experts(send_rows, send_ids)
    sources = got_rows.shape[0] // local_experts
    got = got_rows.reshape(sources, local_experts, capacity, model_width)
    got_cols = pick_columns(got_ids.reshape(-1)).reshape(
        sources, local_experts, capacity, adapt_width
    )
    first_low = (
        jnp.einsum("necd,dr->necr", got, first_down, preferred_element_type=f32) * got_cols
    ).astype(bf16)
    pre = jnp.einsum("necd,edf->necf", got, expert_first, preferred_element_type=f32) + jnp.einsum(
        "necr,rf->necf", first_low, first_up, preferred_element_type=f32
    )
    hidden_val, gelu_back = jax.vjp(lambda values: jax.nn.gelu(values, approximate=False), pre)
    hidden = hidden_val.astype(bf16)
    second_low = (
        jnp.einsum("necf,fr->necr", hidden, second_down, preferred_element_type=f32) * got_cols
    ).astype(bf16)
    part_out = jnp.einsum(
        "necf,efd->necd", hidden, expert_second, preferred_element_type=f32
    ) + jnp.einsum("necr,rd->necd", second_low, second_up, preferred_element_type=f32)
    back_rows = from_experts(part_out.reshape(sources * local_experts, capacity, model_width))
    flat_rows = back_rows.reshape(experts * capacity, model_width)
    fetched = flat_rows[slot_pairs].astype(f32)
    block_output = (middle + jnp.sum(gate_wts[:, :, None] * fetched, axis=1)).astype(bf16)
    grad_out = cotangent.astype(f32)
    grad_gate = jnp.sum(fetched * grad_out[:, None, :], axis=-1) * keep_float
    pair_target = jnp.where(keep_pairs > 0, slot_pairs, experts * capacity)
    slot_gate = jnp.zeros((experts * capacity,), f32).at[pair_target].set(gate_wts, mode="drop")
    grad_pad = jnp.concatenate([cotangent, jnp.zeros((1, model_width), bf16)], axis=0)
    slot_grad = (
        (grad_pad[slot_token].astype(f32) * slot_gate[:, None])
        .astype(bf16)
        .reshape(experts, capacity, model_width)
    )
    got_grad, grad_ids = to_experts(slot_grad, send_ids)
    grad_res = got_grad.reshape(sources, local_experts, capacity, model_width)
    grad_cols = pick_columns(grad_ids.reshape(-1)).reshape(
        sources, local_experts, capacity, adapt_width
    )
    res_low = (
        jnp.einsum("necd,rd->necr", grad_res, second_up, preferred_element_type=f32) * grad_cols
    ).astype(bf16)
    grad_hidden = jnp.einsum(
        "necd,efd->necf", grad_res, expert_second, preferred_element_type=f32
    ) + jnp.einsum("necr,fr->necf", res_low, second_down, preferred_element_type=f32)
    grad_pre = gelu_back(grad_hidden)[0].astype(bf16)
    second_up_part = jnp.einsum("necr,necd->rd", second_low, grad_res, preferred_element_type=f32)
    second_down_part = jnp.einsum("necf,necr->fr", hidden, res_low, preferred_element_type=f32)
    first_up_part = jnp.einsum("necr,necf->rf", first_low, grad_pre, preferred_element_type=f32)
    pre_low = (
        jnp.einsum("necf,rf->necr", grad_pre, first_up, preferred_element_type=f32) * grad_cols
    ).astype(bf16)
    first_down_part = jnp.einsum("necd,necr->dr", got, pre_low, preferred_element_type=f32)
    grad_got = jnp.einsum(
        "necf,edf->necd", grad_pre, expert_first, preferred_element_type=f32
    ) + jnp.einsum("necr,dr->necd", pre_low, first_down, preferred_element_type=f32)
    back_grad = from_experts(grad_got.reshape(sources * local_experts, capacity, model_width))
    back_flat = back_grad.reshape(experts * capacity, model_width)
    grad_mixed = jnp.sum(back_flat[slot_pairs].astype(f32) * keep_float[:, :, None], axis=1)
    grad_picked = gate_prob * (grad_gate - jnp.sum(gate_prob * grad_gate, axis=-1, keepdims=True))
    grad_logits = jnp.sum(chosen * grad_picked[:, :, None], axis=1)
    logit_low = jnp.dot(grad_logits, router_up.astype(f32).T, precision=highest) * pick_cols
    grad_mixed = (
        grad_mixed
        + jnp.dot(grad_logits, router_weight.astype(f32).T, precision=highest)
        + jnp.dot(logit_low, router_down.astype(f32).T, precision=highest)
    )
    router_up_part = jnp.dot(router_low.T, grad_logits, precision=highest)
    router_down_part = jnp.dot(mixed_in.astype(f32).T, logit_low, precision=highest)
    grad_middle = grad_out + norm2_back(grad_mixed)[0]
    grad_branch = grad_middle.astype(bf16)
    project_up_part = jnp.dot(project_low.T, grad_branch, preferred_element_type=f32)
    branch_low = (
        jnp.dot(grad_branch, project_up.T, preferred_element_type=f32) * pick_cols
    ).astype(bf16)
    project_down_part = jnp.dot(attended.T, branch_low, preferred_element_type=f32)
    grad_attended = (
        jnp.dot(grad_branch, project_weight.T, preferred_element_type=f32)
        + jnp.dot(branch_low, project_down.T, preferred_element_type=f32)
    ).astype(bf16)
    grad_heads = grad_attended.reshape(images, seq_len, local_heads, HEAD_DIM)
    again = (
        jnp.einsum("bqhd,bkhd->bhqk", queries, key_rows, preferred_element_type=f32) * score_scale
    )
    probs_again = jnp.exp(again - log_total)
    grad_probs = jnp.einsum("bqhd,bkhd->bhqk", grad_heads, value_rows, preferred_element_type=f32)
    grad_values = jnp.einsum(
        "bhqk,bqhd->bkhd", probs_again.astype(bf16), grad_heads, preferred_element_type=f32
    )
    inner = jnp.sum(probs_again * grad_probs, axis=-1, keepdims=True)
    grad_scores = (probs_again * (grad_probs - inner)).astype(bf16)
    grad_queries = (
        jnp.einsum("bhqk,bkhd->bqhd", grad_scores, key_rows, preferred_element_type=f32)
        * score_scale
    )
    grad_keys = (
        jnp.einsum("bhqk,bqhd->bkhd", grad_scores, queries, preferred_element_type=f32)
        * score_scale
    )
    grad_triple = (
        jnp.stack([grad_queries, grad_keys, grad_values], axis=2)
        .reshape(tok_count, 3 * local_width)
        .astype(bf16)
    )
    triple_up_part = jnp.dot(triple_low.T, grad_triple, preferred_element_type=f32).reshape(
        adapt_width, 3, local_width
    )
    triple_grad_low = jnp.dot(grad_triple, triple_high.T, preferred_element_type=f32) * pick_cols
    triple_down_part = jnp.dot(attn_in.T, triple_grad_low.astype(bf16), preferred_element_type=f32)
    grad_in_part = jnp.dot(grad_triple, triple_flat.T, preferred_element_type=f32) + jnp.dot(
        triple_grad_low.astype(bf16), triple_down.T, preferred_element_type=f32
    )
    grad_attn_in = lax.psum(grad_in_part.astype(jnp.bfloat16), "tensor").astype(jnp.float32)
    input_grad = (grad_middle + norm1_back(grad_attn_in)[0]).astype(bf16)
    (
        triple_up_grad,
        project_down_grad,
        project_up_grad,
        router_down_grad,
        router_up_grad,
        first_up_grad,
        second_down_grad,
    ) = lax.psum(
        (
            triple_up_part,
            project_down_part,
            project_up_part,
            router_down_part,
            router_up_part,
            first_up_part,
            second_down_part,
        ),
        "expert",
    )
    triple_down_grad, first_down_grad, second_up_grad = lax.psum(
        (triple_down_part, first_down_part, second_up_part), ("expert", "tensor")
    )
    return (
        block_output,
        input_grad,
        triple_down_grad,
        triple_up_grad,
        project_down_grad,
        project_up_grad,
        router_down_grad,
        router_up_grad,
        first_down_grad,
        first_up_grad,
        second_down_grad,
        second_up_grad,
    )


def solution(mesh):
    return jax.shard_map(
        body,
        mesh=mesh,
        in_specs=(
            P("expert", None),
            P(),
            P(None, None, "tensor"),
            P("tensor", None),
            P(),
            P(),
            P("expert", None, "tensor"),
            P("expert", "tensor", None),
            P(),
            P(None, None, "tensor"),
            P("tensor", None),
            P(),
            P(),
            P(),
            P(),
            P(None, "tensor"),
            P("tensor", None),
            P(),
            P("expert"),
            P("expert", None),
            P("expert", None),
            P("expert", None),
        ),
        out_specs=(
            P("expert", None),
            P("expert", None),
            P(),
            P(None, None, "tensor"),
            P("tensor", None),
            P(),
            P(),
            P(),
            P(),
            P(None, "tensor"),
            P("tensor", None),
            P(),
        ),
        check_vma=False,
    )
```

profile of v0, /device:TPU:31, one launch (start us, length us, event | category | flops | bytes accessed | tf_op | source)
XLA Modules:
  0.0 1128.6 jit_solution(9242527268222042039)
XLA Ops:
  57.8 8.8 scatter_custom_fusion.3
  66.6 8.8 scatter_custom_fusion.4
  75.4 9.0 scatter_custom_fusion
  84.5 8.8 scatter_custom_fusion.1
  99.0 15.8 %scatter_custom_fusion.2 = s32[3968]{0:T(1024)S(1)} fusion(s32[3152]{0:T(1024)S(1)} %fusion.105, s32[3152]{0:T(1024)S(1)} %pad_add_fusion.1, s32[]{:T(128)} %constant.191.clone.1), kind=kCustom, calls=%fused_computation.210 | custom fusion | bytes 15876 | tf_op jit(solution)/shard_map/scatter | solution.py:41
  114.9 12.4 %gather_fusion.4 = bf16[3968,512]{1,0:T(8,128)(2,1)} fusion(bf16[1577,512]{1,0:T(8,128)(2,1)S(1)} %concatenate.76, s32[4096]{0:T(1024)S(1)} %pad_clamp_fusion.1), kind=kCustom, calls=%fused_computation.4 | custom fusion | bytes 8142336 | tf_op jit(solution)/shard_map/gather | solution.py:193
  136.4 16.0 %scatter_custom_fusion.5 = f32[3968]{0:T(1024)S(1)} fusion(s32[3152]{0:T(1024)} %reshape.722, f32[3152]{0:T(1024)S(1)} %reshape.724, f32[]{:T(128)} %constant.180.clone.1), kind=kCustom, calls=%fused_computation.208 | custom fusion | bytes 16384 | tf_op jit(solution)/shard_map/scatter | solution.py:190
  156.5 5.9 all-to-all-start.3
  164.0 12.4 %gather_fusion.1 = bf16[3968,512]{1,0:T(8,128)(2,1)} fusion(bf16[1577,512]{1,0:T(8,128)(2,1)S(1)} %concatenate.72, s32[4096]{0:T(1024)S(1)} %pad_clamp_fusion.1), kind=kCustom, calls=%fused_computation.1 | custom fusion | bytes 8142336 | tf_op jit(solution)/shard_map/gather | solution.py:160
  176.3 74.9 %all-to-all-done.3 = bf16[16,248,512]{2,1,0:T(8,128)(2,1)} async-done(((bf16[16,248,512]{2,1,0:T(8,128)(2,1)}), bf16[16,248,512]{2,1,0:T(8,128)(2,1)}, u32[]{:S(2)}, u32[]{:S(2)}) %all-to-all-start.3) | async-done | bytes 4063264 | tf_op jit(solution)/shard_map/all_to_all | solution.py:58
  251.2 5.4 all-to-all-start
  256.7 20.9 %gather_fusion.2 = s32[3968]{0:T(1024)S(1)} fusion(s32[1577]{0:T(1024)S(1)} %pad_add_fusion.2, s32[4096]{0:T(1024)S(1)} %pad_clamp_fusion.1), kind=kCustom, calls=%fused_computation.2 | custom fusion | bytes 47616 | tf_op jit(solution)/shard_map/gather | solution.py:162
  278.3 7.6 fusion.19
  285.9 59.6 %all-to-all-done = bf16[16,248,512]{2,1,0:T(8,128)(2,1)} async-done(((bf16[16,248,512]{2,1,0:T(8,128)(2,1)}), bf16[16,248,512]{2,1,0:T(8,128)(2,1)}, u32[]{:S(2)}, u32[]{:S(2)}) %all-to-all-start) | async-done | bytes 4063264 | tf_op jit(solution)/shard_map/all_to_all | solution.py:58
  351.0 7.6 fusion.23
  362.1 6.7 fusion.44
  368.8 19.2 %multiply_convert_fusion = (bf16[8,2,248,512]{3,2,0,1:T(8,128)(2,1)S(1)}, f32[8,2,248,512]{3,2,0,1:T(8,128)}) fusion(f32[8,2,248,512]{3,2,0,1:T(8,128)S(1)} %get-tuple-element.75, u8[2,248,512]{2,1,0:T(8,128)(4,1)S(1)} %get-tuple-element.25, u8[2,248,512]{2,1,0:T(8,128)(4,1)S(1)} %get-tuple-element.24), kind=kLoop, calls=%fused_computation.28 | loop fusion | flops 142213120 | bytes 20824064 | tf_op jit(solution)/shard_map/convert_element_type | solution.py:176
  393.0 8.2 add_convert_fusion
  416.5 149.8 %all-reduce.19.cloned.1.call-done = (bf16[16,248,512]{2,1,0:T(8,128)(2,1)}, bf16[16,248,512]{2,1,0:T(8,128)(2,1)}) async-done(((bf16[16,248,512]{2,1,0:T(8,128)(2,1)}, bf16[16,248,512]{2,1,0:T(8,128)(2,1)}), (bf16[16,248,512]{2,1,0:T(8,128)(2,1)}, bf16[16,248,512]{2,1,0:T(8,128)(2,1)})) %all-reduce.19.cloned.1.call-update) | async-done | bytes 8126480 | tf_op jit(solution)/shard_map/psum | solution.py:65
  566.2 93.9 %all_to_all.30 = bf16[16,248,512]{2,1,0:T(8,128)(2,1)} all-to-all(bf16[16,248,512]{2,1,0:T(8,128)(2,1)} %get-tuple-element.39), channel_id=1, replica_groups=mesh['expert'=8,'tensor'=4] {'expert'}, dimensions={0} | all-to-all | bytes 8126464 | tf_op jit(solution)/shard_map/all_to_all | solution.py:66
  660.1 5.6 all-to-all-start.4
  682.9 13.5 %gather_fusion.3 = bf16[3152,512]{1,0:T(8,128)(2,1)} fusion(bf16[3968,512]{1,0:T(8,128)(2,1)} %bitcast.214, s32[4096]{0:T(1024)S(1)} %pad_clamp_fusion), kind=kCustom, calls=%fused_computation.3 | custom fusion | bytes 6467904 | tf_op jit(solution)/shard_map/gather | solution.py:185
  696.4 7.9 reshape.734
  704.3 21.8 %multiply_reduce_fusion = (f32[1576,2]{1,0:T(8,128)}, f32[1576,512]{1,0:T(8,128)}) fusion(f32[1576,2,512]{2,1,0:T(2,128)} %reshape.734, f32[1576,512]{1,0:T(8,128)} %convert_element_type.195, f32[1576,2]{1,0:T(8,128)S(1)} %copy.191), kind=kLoop, calls=%fused_computation.41 | loop fusion | flops 5645232 | bytes 12935808 | tf_op jit(solution)/shard_map/reduce_sum | solution.py:188
  727.7 26.7 %all-to-all-done.4 = bf16[16,248,512]{2,1,0:T(8,128)(2,1)} async-done(((bf16[16,248,512]{2,1,0:T(8,128)(2,1)}), bf16[16,248,512]{2,1,0:T(8,128)(2,1)}, u32[]{:S(2)}, u32[]{:S(2)}) %all-to-all-start.4) | async-done | bytes 4063264 | tf_op jit(solution)/shard_map/all_to_all | solution.py:66
  754.4 13.1 %gather_fusion.5 = bf16[3152,512]{1,0:T(8,128)(2,1)} fusion(bf16[3968,512]{1,0:T(8,128)(2,1)} %bitcast.41, s32[4096]{0:T(1024)S(1)} %pad_clamp_fusion), kind=kCustom, calls=%fused_computation.5 | custom fusion | bytes 6467904 | tf_op jit(solution)/shard_map/gather | solution.py:221
  767.5 7.9 reshape.735
  776.3 35.1 %multiply_reduce_fusion.1 = f32[1576,512]{1,0:T(8,128)S(1)} fusion(f32[1576,2,512]{2,1,0:T(2,128)} %reshape.735, f32[1576,2]{1,0:T(8,128)S(1)} %copy.207), kind=kLoop, calls=%fused_computation.42 | loop fusion | flops 2420736 | bytes 9695552 | tf_op jit(solution)/shard_map/reduce_sum | solution.py:221
  846.5 14.4 %psum.115 = f32[128,16]{0,1:T(8,128)} all-reduce(f32[128,16]{0,1:T(8,128)S(1)} %fusion.144), channel_id=1, replica_groups=mesh['expert'=8,'tensor'=4] {'expert'}, use_global_device_ids=true, to_apply=%region_38.39 | all-reduce | flops 2048 | bytes 16384 | tf_op jit(solution)/shard_map/psum | solution.py:285
  865.2 18.0 %all-reduce.13.cloned.1.call-done = bf16[1576,512]{1,0:T(8,128)(2,1)} async-done(((bf16[1576,512]{1,0:T(8,128)(2,1)}), bf16[1576,512]{1,0:T(8,128)(2,1)}) %all-reduce.13.cloned.1.call-update) | async-done | bytes 1613840 | tf_op jit(solution)/shard_map/psum | solution.py:275
  891.5 126.2 %all-reduce.15.cloned.1.call-done = (f32[512,128]{1,0:T(8,128)}, f32[512,128]{1,0:T(8,128)}, f32[128,512]{1,0:T(8,128)}) async-done(((f32[512,128]{1,0:T(8,128)}, f32[512,128]{1,0:T(8,128)}, f32[128,512]{1,0:T(8,128)}), (f32[512,128]{1,0:T(8,128)}, f32[512,128]{1,0:T(8,128)}, f32[128,512]{1,0:T(8,128)})) %all-reduce.15.cloned.1.call-update) | async-done | bytes 786448 | tf_op jit(solution)/shard_map/psum | solution.py:297
  1017.7 91.2 %all-reduce.17.cloned.1.call-done = (f32[128,3,128]{2,0,1:T(8,128)}, f32[128,128]{1,0:T(8,128)}, f32[128,512]{1,0:T(8,128)}, f32[512,128]{1,0:T(8,128)}, f32[128,512]{1,0:T(8,128)}, /*index=5*/f32[512,128]{1,0:T(8,128)}) async-done(((f32[128,3,128]{2,0,1:T(8,128)}, f32[128,128]{1,0:T(8,128)}, f32[128,512]{1,0:T(8,128)}, f32[512,128]{1,0:T(8,128)}, f32[128,512]{1,0:T(8,128)}, ...) | async-done | bytes 1310736 | tf_op jit(solution)/shard_map/psum | solution.py:285
  (374 shorter events, 179.6 us)
Async XLA Ops:
  7.2 343.8 %copy-start = (bf16[2,512,512]{2,1,0:T(8,128)(2,1)S(1)}, bf16[2,512,512]{2,1,0:T(8,128)(2,1)}, u32[]{:S(2)}) copy-start(bf16[2,512,512]{2,1,0:T(8,128)(2,1)} %param.30) | copy-start | bytes 3145732
  7.2 120.0 %all-reduce.21.cloned.1.call-start = ((), (), s32[]{:S(2)}) async-start(), calls=%async_computation.9 | async-start | bytes 4034560 | tf_op jit(solution)/shard_map/psum | solution.py:142
  7.3 14.4 %copy-start.89 = (s32[128]{0:T(128)}, s32[128]{0:T(128)S(1)}, u32[]{:S(2)}) copy-start(s32[128]{0:T(128)S(1)} %and_select_fusion) | copy-start | bytes 1540
  114.9 12.4 %copy-start.67 = (bf16[128,512]{1,0:T(8,128)(2,1)S(1)}, bf16[128,512]{1,0:T(8,128)(2,1)}, u32[]{:S(2)}) copy-start(bf16[128,512]{1,0:T(8,128)(2,1)} %param.35) | copy-start | bytes 393220
  114.9 12.4 %copy-start.90 = (s32[128]{0:T(128)S(1)}, s32[128]{0:T(128)}, u32[]{:S(2)}) copy-start(s32[128]{0:T(128)} %copy-done.89) | copy-start | bytes 1540
  156.5 94.7 %all-to-all-start.3 = ((bf16[16,248,512]{2,1,0:T(8,128)(2,1)}), bf16[16,248,512]{2,1,0:T(8,128)(2,1)}, u32[]{:S(2)}, u32[]{:S(2)}) async-start(bf16[16,248,512]{2,1,0:T(8,128)(2,1)} %fusion.1), calls=%async_computation.3 | async-start | bytes 8126464 | tf_op jit(solution)/shard_map/all_to_all | solution.py:58
  251.2 94.3 %all-to-all-start = ((bf16[16,248,512]{2,1,0:T(8,128)(2,1)}), bf16[16,248,512]{2,1,0:T(8,128)(2,1)}, u32[]{:S(2)}, u32[]{:S(2)}) async-start(bf16[16,248,512]{2,1,0:T(8,128)(2,1)} %bitcast.219), calls=%async_computation | async-start | bytes 8126464 | tf_op jit(solution)/shard_map/all_to_all | solution.py:58
  256.7 21.6 %copy-start.30 = (bf16[2,512,512]{2,1,0:T(8,128)(2,1)S(1)}, bf16[2,512,512]{2,1,0:T(8,128)(2,1)}, u32[]{:S(2)}) copy-start(bf16[2,512,512]{2,1,0:T(8,128)(2,1)} %param.31) | copy-start | bytes 3145732
  345.5 13.1 %all-to-all-start.1 = ((s32[8,2,248]{2,1,0:T(2,128)}), s32[8,2,248]{2,1,0:T(2,128)S(1)}, u32[]{:S(2)}, u32[]{:S(2)}) async-start(s32[8,2,248]{2,1,0:T(2,128)} %all_to_all.20), calls=%async_computation.1 | async-start | bytes 32768 | tf_op jit(solution)/shard_map/all_to_all | solution.py:59
  351.0 215.3 %all-reduce.19.cloned.1.call-start = ((), (), s32[]{:S(2)}) async-start(), calls=%async_computation.8 | async-start | bytes 16252928 | tf_op jit(solution)/shard_map/psum | solution.py:65
  362.1 30.9 %slice-start = ((s8[8126464]{0:T(1024)(128)(4,1)}), s8[4194304]{0:T(1024)(128)(4,1)S(1)}, s32[]{:S(2)}) async-start(s8[8126464]{0:T(1024)(128)(4,1)} %bitcast.220), calls=%async_computation.10 | async-start | bytes 8388608
  368.8 19.2 %copy-start.21 = (f32[8,2,248,512]{3,2,0,1:T(8,128)}, f32[8,2,248,512]{3,2,0,1:T(8,128)S(1)}, u32[]{:S(2)}) copy-start(f32[8,2,248,512]{3,2,0,1:T(8,128)S(1)} %get-tuple-element.75) | copy-start | bytes 24379396
  368.8 19.2 %copy-start.60 = (bf16[128,512]{1,0:T(8,128)(2,1)S(1)}, bf16[128,512]{1,0:T(8,128)(2,1)}, u32[]{:S(2)}) copy-start(bf16[128,512]{1,0:T(8,128)(2,1)} %param.41) | copy-start | bytes 393220
  368.8 24.1 %slice-start.1 = ((s8[8126464]{0:T(1024)(128)(4,1)}), s8[3932160]{0:T(1024)(128)(4,1)S(1)}, s32[]{:S(2)}) async-start(s8[8126464]{0:T(1024)(128)(4,1)} %bitcast.220), calls=%async_computation.11 | async-start | bytes 7864320
  388.1 23.2 %copy-start.15 = (bf16[8,2,248,512]{3,2,0,1:T(8,128)(2,1)}, bf16[8,2,248,512]{3,2,0,1:T(8,128)(2,1)S(1)}, u32[]{:S(2)}) copy-start(bf16[8,2,248,512]{3,2,0,1:T(8,128)(2,1)S(1)} %get-tuple-element.47) | copy-start | bytes 12189700
  393.0 8.2 copy-start.102
  660.1 94.3 %all-to-all-start.4 = ((bf16[16,248,512]{2,1,0:T(8,128)(2,1)}), bf16[16,248,512]{2,1,0:T(8,128)(2,1)}, u32[]{:S(2)}, u32[]{:S(2)}) async-start(bf16[16,248,512]{2,1,0:T(8,128)(2,1)} %get-tuple-element.40), calls=%async_computation.4 | async-start | bytes 8126464 | tf_op jit(solution)/shard_map/all_to_all | solution.py:66
  665.8 217.5 %all-reduce.13.cloned.1.call-start = ((), (), s32[]{:S(2)}) async-start(), calls=%async_computation.5 | async-start | bytes 3227648 | tf_op jit(solution)/shard_map/psum | solution.py:275
  704.3 23.2 %copy-start.72 = (f32[1576,2]{0,1:T(2,128)S(1)}, f32[1576,2]{0,1:T(2,128)}, u32[]{:S(2)}) copy-start(f32[1576,2]{0,1:T(2,128)} %get-tuple-element.46) | copy-start | bytes 37828
  704.3 23.3 %copy-start.71 = (s32[1576,2]{0,1:T(2,128)S(1)}, s32[1576,2]{0,1:T(2,128)}, u32[]{:S(2)}) copy-start(s32[1576,2]{0,1:T(2,128)} %param.43) | copy-start | bytes 37828
  727.7 83.8 %copy-start.35 = (f32[1576,16]{0,1:T(8,128)}, f32[1576,16]{0,1:T(8,128)S(1)}, u32[]{:S(2)}) copy-start(f32[1576,16]{0,1:T(8,128)S(1)} %select_reduce_fusion) | copy-start | bytes 302596
  776.3 35.1 %copy-start.78 = (bf16[512,16]{0,1:T(8,128)(2,1)S(1)}, bf16[512,16]{0,1:T(8,128)(2,1)}, u32[]{:S(2)}) copy-start(bf16[512,16]{0,1:T(8,128)(2,1)} %param.29) | copy-start | bytes 49156
  839.3 178.4 %all-reduce.15.cloned.1.call-start = ((), (), s32[]{:S(2)}) async-start(), calls=%async_computation.6 | async-start | bytes 1572864 | tf_op jit(solution)/shard_map/psum | solution.py:297
  845.5 37.7 %copy-start.7 = (bf16[1576,512]{1,0:T(8,128)(2,1)S(1)}, bf16[1576,512]{1,0:T(8,128)(2,1)}, u32[]{:S(2)}) copy-start(bf16[1576,512]{1,0:T(8,128)(2,1)} %param.24) | copy-start | bytes 4841476
  845.5 37.7 %copy-start.55 = (f32[1576]{0:T(1024)S(1)}, f32[1576]{0:T(1024)}, u32[]{:S(2)}) copy-start(f32[1576]{0:T(1024)} %copy-done.54) | copy-start | bytes 18916
  845.5 37.7 %copy-start.84 = (f32[512]{0:T(512)S(1)}, f32[512]{0:T(512)}, u32[]{:S(2)}) copy-start(f32[512]{0:T(512)} %param.25) | copy-start | bytes 6148
  845.5 263.4 %all-reduce.17.cloned.1.call-start = ((), (), s32[]{:S(2)}) async-start(), calls=%async_computation.7 | async-start | bytes 2621440 | tf_op jit(solution)/shard_map/psum | solution.py:285
  860.9 24.9 %copy-start.74 = (f32[1576]{0:T(1024)S(1)}, f32[1576]{0:T(1024)}, u32[]{:S(2)}) copy-start(f32[1576]{0:T(1024)} %copy-done.73) | copy-start | bytes 18916
  860.9 24.9 %copy-start.62 = (f32[1576]{0:T(1024)S(1)}, f32[1576]{0:T(1024)}, u32[]{:S(2)}) copy-start(f32[1576]{0:T(1024)} %copy-done.61) | copy-start | bytes 18916
  888.7 233.1 %copy-start.1 = (bf16[2,512,512]{2,1,0:T(8,128)(2,1)S(1)}, bf16[2,512,512]{2,1,0:T(8,128)(2,1)}, u32[]{:S(2)}) copy-start(bf16[2,512,512]{2,1,0:T(8,128)(2,1)} %param.30) | copy-start | bytes 3145732
  1017.7 103.4 %copy-start.56 = (f32[128,512]{1,0:T(8,128)S(1)}, f32[128,512]{1,0:T(8,128)}, u32[]{:S(2)}) copy-start(f32[128,512]{1,0:T(8,128)} %get-tuple-element.91) | copy-start | bytes 786436
  1108.9 11.5 %copy-start.57 = (f32[512,128]{1,0:T(8,128)S(1)}, f32[512,128]{1,0:T(8,128)}, u32[]{:S(2)}) copy-start(f32[512,128]{1,0:T(8,128)} %get-tuple-element.90) | copy-start | bytes 786436
  (83 other events, 262.1 us)
Sparse Core Ops, SparseCore 0:
  47.0 50.4 all-reduce.20
  416.6 149.6 all-reduce.18
  839.4 43.7 all-reduce.12
  889.2 128.4 all-reduce.14
  1023.6 85.2 all-reduce.16
where the time goes:
time: 1140 us; the launch traced here: 1130 us
  waiting for transfers between devices  546 us (48%)
  local copies, waits for them, and re-layouts  219 us (19%)
  other arithmetic  114 us (10%)
  blocking collectives  108 us (9%)
  matrix products  102 us (9%)
  starting transfers between devices  22.6 us (2%)
  between operations  15.9 us (1%)
    psum x1, waiting for transfers between devices, from_experts(): summed = lax.psum(partial_value.astype(jnp.bfloat16), 'tensor')  150 us
    all_to_all x2, waiting for transfers between devices, to_experts(): lax.all_to_all(row_block, 'expert', split_axis=0, concat_axis=0, tiled=True)  134 us
    psum x1, waiting for transfers between devices, body(): lax.psum((triple_down_part, first_down_part, second_up_part), ('expert',...  126 us
    all_to_all x1, blocking collectives, from_experts(): lax.all_to_all(summed, 'expert', split_axis=0, concat_axis=0, tiled=True)  93.9 us
    psum x1, waiting for transfers between devices, body(): lax.psum((triple_up_part, project_down_part, project_up_part, router_down...  91.2 us
    reduce_sum x1, other arithmetic, body(): jnp.sum(back_flat[slot_pairs].astype(f32) * keep_float[:, :, None], axis=1)  35.1 us
    unnamed x229, local copies, waits for them, and re-layouts  28.4 us
    all_to_all x1, waiting for transfers between devices, from_experts(): lax.all_to_all(summed, 'expert', split_axis=0, concat_axis=0, tiled=True)  26.7 us
  transfers between devices with their start and end apart: 9, of which 7 were waited for; matrix products, arithmetic and copies ran while one was open for 19% of the time, Pallas kernels for 0%

commit v1 on v0

v1 whole, which is shorter than its diff:
```python
import functools

import jax
import jax.numpy as jnp
from jax import lax
from jax.experimental import pallas as pl
from jax.experimental.pallas import tpu as pltpu
from jax.sharding import PartitionSpec as P

HEAD_DIM = 64
TOP = 2
ADAPTERS = 8
RANK = 16
ADAPT = ADAPTERS * RANK
EPS = 1e-06

f32 = jnp.float32
bf16 = jnp.bfloat16
i32 = jnp.int32
MESH = pl.DeviceIdType.MESH
VMEM = pltpu.VMEM


def up(a, b):
    return -(-a // b) * b


def dot(a, b):
    return lax.dot_general(a, b, (((1,), (0,)), ((), ())), preferred_element_type=f32)


def dot_nt(a, b):
    return lax.dot_general(a, b, (((1,), (1,)), ((), ())), preferred_element_type=f32)


def dot_tn(a, b):
    return lax.dot_general(a, b, (((0,), (0,)), ((), ())), preferred_element_type=f32)


def split_high_low(a):
    high = a.astype(bf16)
    return high, (a - high.astype(f32)).astype(bf16)


def dot_fine(a, b):
    high, low = split_high_low(a)
    return dot(high, b) + dot(low, b)


def dot_nt_fine(a, b):
    high, low = split_high_low(a)
    return dot_nt(high, b) + dot_nt(low, b)


def iota(shape, axis):
    return lax.broadcasted_iota(i32, shape, axis)


def to_row(col):
    n = col.shape[0]
    return jnp.sum(jnp.where(iota((n, n), 0) == iota((n, n), 1), col, 0.0), axis=0, keepdims=True)


def to_col(row):
    n = row.shape[1]
    return jnp.sum(jnp.where(iota((n, n), 0) == iota((n, n), 1), row, 0.0), axis=1, keepdims=True)


def pick_of(ids):
    return (ids == iota((1, ADAPT), 1) // RANK).astype(f32)


def whole(count):
    return [pl.BlockSpec(memory_space=VMEM) for _ in range(count)]


def norm_stats(x):
    centre = jnp.mean(x, axis=-1, keepdims=True)
    shifted = x - centre
    scale = lax.rsqrt(jnp.mean(shifted * shifted, axis=-1, keepdims=True) + EPS)
    return shifted * scale, scale


def norm_back(grad, gain, unit, scale):
    g = grad * gain
    return scale * (
        g - jnp.mean(g, axis=-1, keepdims=True) - unit * jnp.mean(g * unit, axis=-1, keepdims=True)
    )


def place_kernel(
    dims, tix, prio, rt, idq, cot, slotc, slotr, cots, cot_pad, rank_s, one_s
):
    nt, seq, seqp, images, experts, cap, capq, cp, width = dims
    t = tix[0]
    tok = prio.shape[1]
    rows = images // nt * seqp
    total = nt * rows
    wide = one_s.shape[-1]
    order = iota((seqp, tok), 1).astype(f32)
    lane = iota((seqp, wide), 1)
    for i in range(images):
        at = pl.ds(i * seqp, seqp)
        token = iota((seqp, 1), 0) + i * seqp
        rank_s[at, :] = jnp.sum(jnp.where(prio[...] == token, order, 0.0), axis=1, keepdims=True)
        r = rt[at, :]
        named = jnp.where(lane < experts, r[:, 0:1], jnp.where(r[:, 1:2] < 0, -1, r[:, 1:2] + experts))
        one_s[at, :] = (named == lane).astype(f32).astype(bf16)
    totals = dot(jnp.ones((8, total), bf16), one_s[...])[0:1]
    rank_rows = [to_row(rank_s[pl.ds(q * rows, rows), :]) for q in range(nt)]
    for q in range(nt):
        at = pl.ds(q * rows, rows)
        mine = rank_s[at, :]
        counts = jnp.zeros((rows, wide), f32)
        for p in range(nt):
            before = (rank_rows[p] < mine).astype(f32).astype(bf16)
            counts = counts + dot(before, one_s[pl.ds(p * rows, rows), :])
        lane = iota((rows, wide), 1)
        r = rt[at, :]
        hot = one_s[at, :].astype(f32) * counts
        first = jnp.sum(jnp.where(lane < experts, hot, 0.0), axis=1, keepdims=True)
        second = jnp.sum(
            jnp.where(lane < experts, 0.0, hot)
            + jnp.where((lane < experts) & (r[:, 1:2] == lane), totals, 0.0),
            axis=1,
            keepdims=True,
        )
        for k, pos in ((0, first), (1, second)):
            e = r[:, k : k + 1]
            place = pos.astype(i32)
            kept = (e >= 0) & (place < cap) & (lax.rem(place, nt) == t)
            slot = jnp.where(kept, e * cp + lax.div(place, nt), -1)
            slotc[q, :, k : k + 1] = slot
            slotr[q, k : k + 1, :] = to_row(slot.astype(f32)).astype(i32)
    for i in range(images):
        start = i * seq // 16 * 16
        stop = min(start + up(seq, 16) + 16, tok)
        src = iota((seqp, stop - start), 1) + start
        row = iota((seqp, stop - start), 0)
        sel = ((src == row + i * seq) & (row < seq)).astype(f32).astype(bf16)
        cot_pad[pl.ds(i * seqp, seqp), :] = dot(sel, cot[start:stop, :]).astype(bf16)
    n_out, block = cots.shape[0], cots.shape[1]
    step = max(1, 256 // block)
    ids = [idq[q] for q in range(nt)]

    def send(d, carry):
        s = iota((step * block, 1), 0) + d * (step * block)
        acc = jnp.zeros((step * block, width), f32)
        idc = jnp.zeros((step * block, 1), f32)
        for q in range(nt):
            g = (slotr[q, 0:1, :] == s) | (slotr[q, 1:2, :] == s)
            idc = idc + jnp.sum(jnp.where(g, ids[q], 0.0), axis=1, keepdims=True)
            acc = acc + dot(g.astype(f32).astype(bf16), cot_pad[pl.ds(q * rows, rows), :])
        for b in range(step):
            part = acc[b * block : (b + 1) * block]
            idr = to_row(idc[b * block : (b + 1) * block])
            row = iota((block, block), 0)
            cots[d * step + b, :, 0:block] = jnp.where(row == capq, idr, part[:, 0:block]).astype(bf16)
            cots[d * step + b, :, block:] = part[:, block:].astype(bf16)
        return carry

    lax.fori_loop(0, n_out // step, send, 0)


def attend_kernel(
    dims, tix, x_ref, gain1, wt, tup, tdn, pw, pd, pup, gain2, idq,
    mixed, middle, triple, attended, tlow, plow, attn_in, xs,
):
    nt, seq, seqp, images = dims
    per = images // nt
    rows = per * seqp
    tok = x_ref.shape[0]
    lw = wt.shape[2] // 3
    for li in range(per):
        base = (tix[0] * per + li) * seq
        row = iota((seqp, tok), 0)
        sel = ((iota((seqp, tok), 1) == row + base) & (row < seq)).astype(f32).astype(bf16)
        xs[pl.ds(li * seqp, seqp), :] = dot(sel, x_ref[...])
    pick = pick_of(idq[...])
    unit, _ = norm_stats(xs[...])
    normed = (unit * gain1[...]).astype(bf16)
    attn_in[...] = normed
    low = (dot(normed, tdn[...]) * pick).astype(bf16)
    tlow[...] = low
    head_of = iota((1, lw), 1) // HEAD_DIM
    key_ok = iota((1, seqp), 1) < seq

    def piece(p, carry):
        triple[p] = (dot(normed, wt[p]) + dot(low, tup[p])).astype(bf16)
        for li in range(per):
            at = pl.ds(li * seqp, seqp)
            q = triple[p, at, 0:lw]
            k = triple[p, at, lw : 2 * lw]
            v = triple[p, at, 2 * lw : 3 * lw]
            acc = jnp.zeros((seqp, lw), f32)
            for h in range(lw // HEAD_DIM):
                on = head_of == h
                s = dot_nt(jnp.where(on, q, 0.0).astype(bf16), k) * HEAD_DIM**-0.5
                s = jnp.where(key_ok, s, -jnp.inf)
                e = jnp.exp(s - jnp.max(s, axis=1, keepdims=True))
                probs = (e / jnp.sum(e, axis=1, keepdims=True)).astype(bf16)
                acc = acc + dot(probs, jnp.where(on, v, 0.0).astype(bf16))
            attended[p, at, :] = acc.astype(bf16)
        return carry

    lax.fori_loop(0, nt, piece, 0)
    psum = jnp.zeros((rows, ADAPT), f32)
    branch = jnp.zeros((rows, pup.shape[1]), f32)
    for p in range(nt):
        psum = psum + dot(attended[p], pd[p])
        branch = branch + dot(attended[p], pw[p])
    low2 = (psum * pick).astype(bf16)
    plow[...] = low2
    mid = xs[...] + branch + dot(low2, pup[...])
    middle[...] = mid
    unit2, _ = norm_stats(mid)
    mixed[...] = (unit2 * gain2[...]).astype(bf16)


def gates_of(mixed, rt, ids, rw, rd, ru):
    pick = pick_of(ids)
    low = dot(mixed, rd) * pick
    logits = dot(mixed, rw) + dot_fine(low, ru)
    lane = iota((1, rw.shape[1]), 1)
    first = jnp.sum(jnp.where(rt[:, 0:1] == lane, logits, 0.0), axis=1, keepdims=True)
    second = jnp.sum(jnp.where(rt[:, 1:2] == lane, logits, 0.0), axis=1, keepdims=True)
    top = jnp.maximum(first, second)
    a = jnp.exp(first - top)
    b = jnp.exp(second - top)
    return a / (a + b), b / (a + b), low, pick


def dispatch_kernel(dims, mixed, rt, idc, slotc, slotr, rw, rd, ru, sends, gate_s):
    nt, capq = dims
    rows = mixed.shape[1]
    for q in range(nt):
        at = pl.ds(q * rows, rows)
        a, b, _, _ = gates_of(mixed[q], rt[at, :], idc[at, :], rw[...], rd[...], ru[...])
        gate_s[q, 0] = a
        gate_s[q, 1] = b
    n_out, block, width = sends.shape
    step = max(1, 256 // block)

    def send(d, carry):
        s = iota((step * block, 1), 0) + d * (step * block)
        acc = jnp.zeros((step * block, width), f32)
        for q in range(nt):
            g = (slotr[q, 0:1, :] == s) | (slotr[q, 1:2, :] == s)
            acc = acc + dot(g.astype(f32).astype(bf16), mixed[q])
        sr = iota((1, step * block), 1) + d * (step * block)
        gate = jnp.zeros((1, step * block), f32)
        for q in range(nt):
            for k in range(TOP):
                gate = gate + jnp.sum(
                    jnp.where(slotc[q, :, k : k + 1] == sr, gate_s[q, k], 0.0), axis=0, keepdims=True
                )
        high = gate.astype(bf16).astype(f32)
        low = gate - high
        for b in range(step):
            part = acc[b * block : (b + 1) * block]
            row = iota((block, block), 0)
            head = jnp.where(row == capq, high[:, b * block : (b + 1) * block], part[:, 0:block])
            head = jnp.where(row == capq + 1, low[:, b * block : (b + 1) * block], head)
            sends[d * step + b, :, 0:block] = head.astype(bf16)
            sends[d * step + b, :, block:] = part[:, block:].astype(bf16)
        return carry

    lax.fori_loop(0, n_out // step, send, 0)


def erf_parts(pre):
    cdf = 0.5 * (1.0 + lax.erf(pre * 0.7071067811865476))
    return pre * cdf, cdf + pre * (jnp.exp(-0.5 * pre * pre) * 0.3989422804014327)


def expert_kernel(
    dims, got, cot, w1, w2, fdn, fup, sdn, sup, rets, grads,
    sent_s, sg_s, hid_s, dg_s, low_s, gh_s, acc_fd, acc_fu, acc_sd, acc_su,
):
    nt, local, capq, cp = dims
    n, block, width = got.shape
    ffq = w1.shape[3]
    rows = n * cp
    row_in = iota((rows, 1), 0)
    real = lax.rem(row_in, cp) < capq
    acc_fd[...] = jnp.zeros_like(acc_fd)
    acc_fu[...] = jnp.zeros_like(acc_fu)
    acc_sd[...] = jnp.zeros_like(acc_sd)
    acc_su[...] = jnp.zeros_like(acc_su)
    for e in range(local):
        at = pl.ds(e * cp, cp)
        sent = jnp.where(real, got[:, at, :].reshape(rows, width).astype(f32), 0.0).astype(bf16)
        cots = jnp.where(real, cot[:, at, :].reshape(rows, width).astype(f32), 0.0)
        ids, gates = [], []
        row = iota((cp, block), 0) + e * cp
        diag = row == iota((cp, block), 1)
        for m in range(n):
            idr = cot[m, capq : capq + 1, 0:block].astype(f32)
            gr = got[m, capq : capq + 1, 0:block].astype(f32) + got[
                m, capq + 1 : capq + 2, 0:block
            ].astype(f32)
            ids.append(jnp.sum(jnp.where(diag, idr, 0.0), axis=1, keepdims=True))
            gates.append(jnp.sum(jnp.where(diag, gr, 0.0), axis=1, keepdims=True))
        idc = jnp.concatenate(ids, axis=0).astype(i32)
        gate = jnp.concatenate(gates, axis=0)
        pick = pick_of(idc)
        sent_s[...] = sent
        sgrad = (gate * cots).astype(bf16)
        sg_s[...] = sgrad
        first_low = (dot(sent, fdn[...]) * pick).astype(bf16)
        low_s[0] = first_low
        g2low = (dot_nt(sgrad, sup[...]) * pick).astype(bf16)
        low_s[1] = g2low

        def ahead(c, carry):
            second, res = carry
            pre = dot(sent_s[...], w1[c, e]) + dot(low_s[0], fup[c])
            act, slope = erf_parts(pre)
            hid = act.astype(bf16)
            hid_s[c] = hid
            dg_s[c] = slope
            return second + dot(hid, sdn[c]), res + dot(hid, w2[c, e])

        second, res = lax.fori_loop(
            0, nt, ahead, (jnp.zeros((rows, ADAPT), f32), jnp.zeros((rows, width), f32))
        )
        second_low = (second * pick).astype(bf16)
        res = (res + dot(second_low, sup[...])).astype(bf16).astype(f32)
        grad_gate = jnp.sum(res * cots, axis=1, keepdims=True)
        out = gate * res
        for m in range(n):
            part = out[m * cp : (m + 1) * cp]
            rets[m, 0, at, :] = part.astype(bf16)
            gg = jnp.sum(
                jnp.where(diag, grad_gate[m * cp : (m + 1) * cp], 0.0), axis=0, keepdims=True
            )
            gh_s[m : m + 1, :] = gg if e == 0 else gh_s[m : m + 1, :] + gg
        acc_su[...] += dot_tn(second_low, sgrad)

        def back(c, carry):
            low1, gsent = carry
            ghid = dot_nt(sg_s[...], w2[c, e]) + dot_nt(low_s[1], sdn[c])
            gpre = (ghid * dg_s[c]).astype(bf16)
            acc_fu[c] += dot_tn(low_s[0], gpre)
            acc_sd[c] += dot_tn(low_s[1], hid_s[c])
            return low1 + dot_nt(gpre, fup[c]), gsent + dot_nt(gpre, w1[c, e])

        low1, gsent = lax.fori_loop(
            0, nt, back, (jnp.zeros((rows, ADAPT), f32), jnp.zeros((rows, width), f32))
        )
        g1low = (low1 * pick).astype(bf16)
        gsent = gsent + dot_nt(g1low, fdn[...])
        acc_fd[...] += dot_tn(g1low, sent)
        for m in range(n):
            rets[m, 1, at, :] = gsent[m * cp : (m + 1) * cp].astype(bf16)
    for m in range(n):
        gg = gh_s[m : m + 1, :]
        high = gg.astype(bf16).astype(f32)
        row = iota((16, block), 0)
        base = capq // 16 * 16
        old = rets[m, 0, pl.ds(base, 16), 0:block].astype(f32)
        new = jnp.where(row == capq - base, high, jnp.where(row == capq + 1 - base, gg - high, old))
        rets[m, 0, pl.ds(base, 16), 0:block] = new.astype(bf16)
    quarter = width // nt
    for q in range(nt):
        off = 0
        for c in range(ffq // 128):
            grads[q, off : off + 128, :] = acc_fu[q, :, c * 128 : (c + 1) * 128].astype(bf16)
            off += 128
        grads[q, off : off + ffq, :] = acc_sd[q].T.astype(bf16)
        off += ffq
        grads[q, off : off + quarter, :] = acc_fd[:, q * quarter : (q + 1) * quarter].T.astype(bf16)
        off += quarter
        for c in range(width // 128):
            at = slice(q * (ADAPT // nt), (q + 1) * (ADAPT // nt))
            grads[q, off : off + ADAPT // nt, :] = acc_su[at, c * 128 : (c + 1) * 128].astype(bf16)
            off += ADAPT // nt


def combine_kernel(dims, got, slotc, slotr, res, grad, gg, gcol, rows_s):
    nt, capq = dims
    n, _, block, width = got.shape
    rows = slotc.shape[1]
    for d in range(n):
        gr = got[d, 0, capq : capq + 1, 0:block].astype(f32) + got[
            d, 0, capq + 1 : capq + 2, 0:block
        ].astype(f32)
        gcol[d * block : (d + 1) * block, :] = to_col(gr)
        for j in range(2):
            rows_s[j, d * block : (d + 1) * block, :] = got[d, j]
    slots = n * block
    for q in range(nt):
        s = iota((1, slots), 1)
        g = ((slotc[q, :, 0:1] == s) | (slotc[q, :, 1:2] == s)).astype(f32).astype(bf16)
        grad[q] = dot(g, rows_s[1]).astype(bf16)
        res[q] = dot(g, rows_s[0]).astype(bf16)
        sc = iota((slots, 1), 0)
        for k in range(TOP):
            gg[q, k : k + 1, :] = jnp.sum(
                jnp.where(slotr[q, k : k + 1, :] == sc, gcol[...], 0.0), axis=0, keepdims=True
            )


def back_kernel(
    dims, tix, cot_ref, gmix, ggate, mixed, middle, triple, attended, tlow, plow, attn_in, x_ref,
    gain1, gain2, wt, tup, tdn, pw, pd, pup, rw, rd, ru, rt, idq,
    igrad, grads, xs, gt_s, ga_s, acc_in, acc_low,
):
    nt, seq, seqp, images = dims
    per = images // nt
    tok = x_ref.shape[0]
    width = x_ref.shape[1]
    lw = wt.shape[2] // 3
    rows = per * seqp
    quarter = width // nt
    for li in range(per):
        base = (tix[0] * per + li) * seq
        row = iota((seqp, tok), 0)
        sel = ((iota((seqp, tok), 1) == row + base) & (row < seq)).astype(f32).astype(bf16)
        at = pl.ds(li * seqp, seqp)
        xs[0, at, :] = dot(sel, x_ref[...])
        xs[1, at, :] = dot(sel, cot_ref[...])
    r = rt[...]
    prob0, prob1, rlow, pick = gates_of(mixed[...], r, idq[...], rw[...], rd[...], ru[...])
    gg0 = to_col(ggate[0:1, :])
    gg1 = to_col(ggate[1:2, :])
    inner = prob0 * gg0 + prob1 * gg1
    lane = iota((1, rw.shape[1]), 1)
    glog = jnp.where(r[:, 0:1] == lane, prob0 * (gg0 - inner), 0.0) + jnp.where(
        r[:, 1:2] == lane, prob1 * (gg1 - inner), 0.0
    )
    llow = dot_nt_fine(glog, ru[...]) * pick
    gm = gmix[...].astype(f32) + dot_nt_fine(glog, rw[...]) + dot_nt_fine(llow, rd[...])
    router_up = dot_tn(rlow.astype(bf16), glog.astype(bf16))
    router_down = dot_tn(mixed[...], llow.astype(bf16))
    unit2, scale2 = norm_stats(middle[...])
    gmid = xs[1] + norm_back(gm, gain2[...], unit2, scale2)
    xs[1] = gmid
    gbranch = gmid.astype(bf16)
    project_up = dot_tn(plow[...], gbranch)
    blow = (dot_nt(gbranch, pup[...]) * pick).astype(bf16)
    for p in range(nt):
        ga_s[p] = (dot_nt(gbranch, pw[p]) + dot_nt(blow, pd[p])).astype(bf16)
    head_of = iota((1, lw), 1) // HEAD_DIM
    key_ok = iota((1, seqp), 1) < seq
    acc_in[...] = jnp.zeros_like(acc_in)
    acc_low[...] = jnp.zeros_like(acc_low)

    def piece(p, carry):
        for li in range(per):
            at = pl.ds(li * seqp, seqp)
            q = triple[p, at, 0:lw]
            k = triple[p, at, lw : 2 * lw]
            v = triple[p, at, 2 * lw : 3 * lw]
            ga = ga_s[p, at, :]
            gq = jnp.zeros((seqp, lw), f32)
            gk = jnp.zeros((seqp, lw), f32)
            gv = jnp.zeros((seqp, lw), f32)
            for h in range(lw // HEAD_DIM):
                on = head_of == h
                qm = jnp.where(on, q, 0.0).astype(bf16)
                km = jnp.where(on, k, 0.0).astype(bf16)
                gam = jnp.where(on, ga, 0.0).astype(bf16)
                s = dot_nt(qm, k) * HEAD_DIM**-0.5
                s = jnp.where(key_ok, s, -jnp.inf)
                e = jnp.exp(s - jnp.max(s, axis=1, keepdims=True))
                probs = e / jnp.sum(e, axis=1, keepdims=True)
                gp = dot_nt(gam, v)
                ds = (probs * (gp - jnp.sum(probs * gp, axis=1, keepdims=True))).astype(bf16)
                gq = gq + dot(ds, km)
                gk = gk + dot_tn(ds, qm)
                gv = gv + dot_tn(probs.astype(bf16), gam)
            gt_s[at, 0:lw] = (gq * HEAD_DIM**-0.5).astype(bf16)
            gt_s[at, lw : 2 * lw] = (gk * HEAD_DIM**-0.5).astype(bf16)
            gt_s[at, 2 * lw : 3 * lw] = gv.astype(bf16)
        gt = gt_s[...]
        acc_low[...] += dot_nt(gt, tup[p])
        acc_in[...] += dot_nt(gt, wt[p])
        tu = dot_tn(tlow[...], gt)
        for c in range(3 * lw // 128):
            grads[p, c * 128 : (c + 1) * 128, :] = tu[:, c * 128 : (c + 1) * 128].astype(bf16)
        off = 3 * lw
        grads[p, off : off + lw, :] = dot_tn(attended[p], blow).astype(bf16)
        return carry

    lax.fori_loop(0, nt, piece, 0)
    tglow = (acc_low[...] * pick).astype(bf16)
    gin = acc_in[...] + dot_nt(tglow, tdn[...])
    triple_down = dot_tn(attn_in[...], tglow)
    unit1, scale1 = norm_stats(xs[0])
    igrad[...] = (xs[1] + norm_back(gin, gain1[...], unit1, scale1)).astype(bf16)
    share = ADAPT // nt
    for q in range(nt):
        off = 4 * lw
        at = slice(q * quarter, (q + 1) * quarter)
        grads[q, off : off + quarter, :] = triple_down[at].astype(bf16)
        off += quarter
        grads[q, off : off + quarter, :] = router_down[at].astype(bf16)
        off += quarter
        at = slice(q * share, (q + 1) * share)
        for c in range(width // 128):
            grads[q, off : off + share, :] = project_up[at, c * 128 : (c + 1) * 128].astype(bf16)
            off += share
        ex = rw.shape[1]
        if ex < 128:
            grads[q, off : off + share, :] = jnp.zeros((share, 128), bf16)
        grads[q, off : off + share, 0:ex] = router_up[at].astype(bf16)


def greet(peers):
    barrier = pltpu.get_barrier_semaphore()
    for peer in peers:
        pl.semaphore_signal(barrier, 1, device_id=peer, device_id_type=MESH)
    pl.semaphore_wait(barrier, len(peers))


def remote(src, dst, send, recv, peer):
    return pltpu.make_async_remote_copy(
        src_ref=src, dst_ref=dst, send_sem=send, recv_sem=recv, device_id=peer, device_id_type=MESH
    )


def swap_kernel(n, x_ref, o_ref, send, recv, here):
    e = lax.axis_index("expert")
    t = lax.axis_index("tensor")
    greet([(lax.rem(e + d, n), t) for d in range(1, n)])
    copies = []
    for d in range(1, n):
        p = lax.rem(e + d, n)
        copies.append(remote(x_ref.at[p], o_ref.at[e], send.at[d], recv.at[d], (p, t)))
        copies[-1].start()
    own = pltpu.make_async_copy(x_ref.at[e], o_ref.at[e], here)
    own.start()
    for copy in copies:
        copy.wait()
    own.wait()


def swap(x, n, ident):
    return pl.pallas_call(
        functools.partial(swap_kernel, n),
        out_shape=jax.ShapeDtypeStruct(x.shape, x.dtype),
        in_specs=whole(1),
        out_specs=pl.BlockSpec(memory_space=VMEM),
        scratch_shapes=[
            pltpu.SemaphoreType.DMA((n,)),
            pltpu.SemaphoreType.DMA((n,)),
            pltpu.SemaphoreType.DMA,
        ],
        compiler_params=pltpu.CompilerParams(collective_id=ident, has_side_effects=True),
    )(x)


def gather_kernel(nt, x_ref, o_ref, send, recv, here):
    e = lax.axis_index("expert")
    t = lax.axis_index("tensor")
    far = jnp.bitwise_xor(t, 2)
    near = jnp.bitwise_xor(t, 1)
    greet([(e, far), (e, near)])
    out = remote(x_ref, o_ref.at[t], send.at[0], recv.at[0], (e, far))
    side = remote(x_ref, o_ref.at[t], send.at[1], recv.at[1], (e, near))
    out.start()
    side.start()
    own = pltpu.make_async_copy(x_ref, o_ref.at[t], here)
    own.start()
    out.wait_recv()
    relay = remote(o_ref.at[far], o_ref.at[far], send.at[2], recv.at[2], (e, near))
    relay.start()
    out.wait_send()
    side.wait()
    relay.wait()
    own.wait()


def gather(x, nt, ident):
    return pl.pallas_call(
        functools.partial(gather_kernel, nt),
        out_shape=jax.ShapeDtypeStruct((nt,) + x.shape, x.dtype),
        in_specs=whole(1),
        out_specs=pl.BlockSpec(memory_space=VMEM),
        scratch_shapes=[
            pltpu.SemaphoreType.DMA((3,)),
            pltpu.SemaphoreType.DMA((3,)),
            pltpu.SemaphoreType.DMA,
        ],
        compiler_params=pltpu.CompilerParams(collective_id=ident, has_side_effects=True),
    )(x)


def gather_early(x, nt):
    t = lax.axis_index("tensor")
    near = lax.ppermute(x, "tensor", [(i, i ^ 1) for i in range(nt)])
    far = lax.ppermute(x, "tensor", [(i, i ^ 2) for i in range(nt)])
    cross = lax.ppermute(far, "tensor", [(i, i ^ 1) for i in range(nt)])
    out = jnp.zeros((nt,) + x.shape, x.dtype)
    for mask, part in ((0, x), (1, near), (2, far), (3, cross)):
        out = lax.dynamic_update_index_in_dim(out, part, jnp.bitwise_xor(t, mask), 0)
    return out


def scatter_kernel(nt, grad, res, gg, ograd, ores, ogg, keep_g, keep_r, keep_k, in1, in1r, in1k, in2, in2r, in2k, send, recv):
    e = lax.axis_index("expert")
    t = lax.axis_index("tensor")
    far = jnp.bitwise_xor(t, 2)
    near = jnp.bitwise_xor(t, 1)
    nearfar = jnp.bitwise_xor(t, 3)
    greet([(e, far), (e, near)])
    first = []
    for i, (src, dst) in enumerate(((grad, in1), (gg, in1k), (res, in1r))):
        for j, q in enumerate((nearfar, near)):
            copy = remote(src.at[q], dst.at[j], send.at[2 * i + j], recv.at[2 * i + j], (e, near))
            copy.start()
            first.append(copy)
    second = []
    for i, (src, one, keep, two) in enumerate(
        ((grad, in1, keep_g, in2), (gg, in1k, keep_k, in2k), (res, in1r, keep_r, in2r))
    ):
        first[2 * i].wait()
        keep[...] = (src[far].astype(f32) + one[0].astype(f32)).astype(keep.dtype)
        copy = remote(keep, two, send.at[6 + i], recv.at[6 + i], (e, far))
        copy.start()
        second.append(copy)
    for i, (src, one, two, out) in enumerate(
        ((grad, in1, in2, ograd), (gg, in1k, in2k, ogg), (res, in1r, in2r, ores))
    ):
        first[2 * i + 1].wait()
        mine = src[t].astype(f32) + one[1].astype(f32)
        second[i].wait()
        out[...] = (mine + two[...].astype(f32)).astype(out.dtype)


def scatter_sums(grad, res, gg, nt, ident):
    one = grad.shape[1:]
    small = gg.shape[1:]
    return pl.pallas_call(
        functools.partial(scatter_kernel, nt),
        out_shape=[
            jax.ShapeDtypeStruct(one, f32),
            jax.ShapeDtypeStruct(one, f32),
            jax.ShapeDtypeStruct(small, f32),
        ],
        in_specs=whole(3),
        out_specs=whole(3),
        scratch_shapes=[
            VMEM(one, bf16), VMEM(one, bf16), VMEM(small, f32),
            VMEM((2,) + one, bf16), VMEM((2,) + one, bf16), VMEM((2,) + small, f32),
            VMEM(one, bf16), VMEM(one, bf16), VMEM(small, f32),
            pltpu.SemaphoreType.DMA((9,)),
            pltpu.SemaphoreType.DMA((9,)),
        ],
        compiler_params=pltpu.CompilerParams(collective_id=ident, has_side_effects=True),
    )(grad, res, gg)


def reduce_kernel(nt, ne, first_rows, rep, x_ref, o_ref, rep_ref, in1, keep, in2, mine, parts, total, send, recv):
    e = lax.axis_index("expert")
    t = lax.axis_index("tensor")
    far = jnp.bitwise_xor(t, 2)
    near = jnp.bitwise_xor(t, 1)
    nearfar = jnp.bitwise_xor(t, 3)
    greet([(e, far), (e, near)] + [(lax.rem(e + d, ne), t) for d in range(1, ne)])
    a = remote(x_ref.at[nearfar], in1.at[0], send.at[0], recv.at[0], (e, near))
    b = remote(x_ref.at[near], in1.at[1], send.at[1], recv.at[1], (e, near))
    a.start()
    b.start()
    a.wait()
    keep[...] = (x_ref[far].astype(f32) + in1[0].astype(f32)).astype(bf16)
    c = remote(keep, in2, send.at[2], recv.at[2], (e, far))
    c.start()
    b.wait()
    own = x_ref[t].astype(f32) + in1[1].astype(f32)
    c.wait()
    mine[...] = (own + in2[...].astype(f32)).astype(bf16).reshape(mine.shape)
    out = []
    for d in range(1, ne):
        p = lax.rem(e + d, ne)
        out.append(remote(mine.at[p], parts.at[d - 1], send.at[2 + d], recv.at[2 + d], (p, t)))
        out[-1].start()
    acc = mine[e].astype(f32)
    for d in range(1, ne):
        out[d - 1].wait()
        acc = acc + parts[d - 1].astype(f32)
    total[e] = acc.astype(bf16)
    back = []
    for d in range(1, ne):
        p = lax.rem(e + d, ne)
        k = 1 + ne + d
        back.append(remote(total.at[e], total.at[e], send.at[k], recv.at[k], (p, t)))
        back[-1].start()
    for copy in back:
        copy.wait()
    full = total[...].reshape(o_ref.shape)
    o_ref[...] = full
    rep_ref[t] = full[first_rows : first_rows + rep]
    k = 1 + 2 * ne
    out = remote(rep_ref.at[t], rep_ref.at[t], send.at[k], recv.at[k], (e, far))
    side = remote(rep_ref.at[t], rep_ref.at[t], send.at[k + 1], recv.at[k + 1], (e, near))
    out.start()
    side.start()
    out.wait_recv()
    relay = remote(rep_ref.at[far], rep_ref.at[far], send.at[k + 2], recv.at[k + 2], (e, near))
    relay.start()
    out.wait_send()
    side.wait()
    relay.wait()


def reduce_all(x, nt, ne, first_rows, rep, ident):
    rows = x.shape[1]
    chunk = rows // ne
    return pl.pallas_call(
        functools.partial(reduce_kernel, nt, ne, first_rows, rep),
        out_shape=[
            jax.ShapeDtypeStruct((rows, 128), bf16),
            jax.ShapeDtypeStruct((nt, rep, 128), bf16),
        ],
        in_specs=whole(1),
        out_specs=whole(2),
        scratch_shapes=[
            VMEM((2, rows, 128), bf16),
            VMEM((rows, 128), bf16),
            VMEM((rows, 128), bf16),
            VMEM((ne, chunk, 128), bf16),
            VMEM((ne - 1, chunk, 128), bf16),
            VMEM((ne, chunk, 128), bf16),
            pltpu.SemaphoreType.DMA((4 + 2 * ne,)),
            pltpu.SemaphoreType.DMA((4 + 2 * ne,)),
        ],
        compiler_params=pltpu.CompilerParams(collective_id=ident, has_side_effects=True),
    )(x)


def body(
    inputs, gain_attend, triple_weight, project_weight, gain_mixture, router_weight, expert_first,
    expert_second, triple_down, triple_up, project_down, project_up, router_down, router_up,
    first_down, first_up, second_down, second_up, adapter_index, routes, priority, cotangent,
):
    ne = lax.axis_size("expert")
    nt = lax.axis_size("tensor")
    tok, width = inputs.shape
    images = adapter_index.shape[0]
    seq = tok // images
    seqp = up(seq, 16)
    per = images // nt
    rows = per * seqp
    experts = router_weight.shape[1]
    local = expert_first.shape[0]
    ffq = expert_first.shape[2]
    lw = triple_weight.shape[2]
    cap = nt * ((5 * tok * TOP + 4 * nt * experts - 1) // (4 * nt * experts))
    capq = cap // nt
    cp = up(capq + 2, 16)
    block = local * cp
    t = lax.axis_index("tensor")
    tix = t.astype(i32).reshape(1)
    smem = pl.BlockSpec(memory_space=pltpu.SMEM)

    wt_q = triple_weight.reshape(width, 3 * lw)
    att = jnp.concatenate(
        [wt_q, triple_up.reshape(ADAPT, 3 * lw)], axis=0
    )
    prj = jnp.concatenate([project_weight, project_down], axis=1)
    att_all = gather_early(att, nt)
    prj_all = gather_early(prj, nt)
    w1_all = gather_early(expert_first, nt)
    w2_all = gather_early(expert_second, nt)
    low_all = gather_early(jnp.stack([first_up.reshape(ADAPT, ffq // 128, 128).swapaxes(0, 1).reshape(ffq, 128), second_down]), nt)
    wt_all = att_all[:, :width]
    tup_all = att_all[:, width:]
    pw_all = prj_all[:, :, :width]
    pd_all = prj_all[:, :, width:]
    fup_all = low_all[:, 0].reshape(nt, ffq // 128, ADAPT, 128).swapaxes(1, 2).reshape(nt, ADAPT, ffq)
    sdn_all = low_all[:, 1]

    prio = priority + (seqp - seq) * (priority // seq)
    rt = jnp.pad(
        routes.reshape(images, seq, TOP), ((0, 0), (0, seqp - seq), (0, 0)), constant_values=-1
    ).reshape(images * seqp, TOP)
    ids = jnp.repeat(adapter_index, seqp, total_repeat_length=images * seqp)
    idc = ids.reshape(-1, 1)
    idq = lax.dynamic_slice(idc, (t * rows, 0), (rows, 1))
    rtq = lax.dynamic_slice(rt, (t * rows, 0), (rows, TOP))
    gain1 = gain_attend.reshape(1, width)
    gain2 = gain_mixture.reshape(1, width)

    wide = up(2 * experts, 128)
    slotc, slotr, cots = pl.pallas_call(
        functools.partial(
            place_kernel, (nt, seq, seqp, images, experts, cap, capq, cp, width)
        ),
        out_shape=[
            jax.ShapeDtypeStruct((nt, rows, TOP), i32),
            jax.ShapeDtypeStruct((nt, TOP, rows), i32),
            jax.ShapeDtypeStruct((ne, block, width), bf16),
        ],
        in_specs=[smem] + whole(4),
        out_specs=whole(3),
        scratch_shapes=[
            VMEM((images * seqp, width), bf16),
            VMEM((images * seqp, 1), f32),
            VMEM((images * seqp, wide), bf16),
        ],
        name="place",
    )(tix, prio, rt, ids.astype(f32).reshape(nt, 1, rows), cotangent)
    got_cot = lax.all_to_all(cots, "expert", 0, 0, tiled=True)

    row_f = jax.ShapeDtypeStruct((rows, width), f32)
    row_b = jax.ShapeDtypeStruct((rows, width), bf16)
    low_b = jax.ShapeDtypeStruct((rows, ADAPT), bf16)
    mixed, middle, triple, attended, tlow, plow, attn_in = pl.pallas_call(
        functools.partial(attend_kernel, (nt, seq, seqp, images)),
        out_shape=[
            row_b,
            row_f,
            jax.ShapeDtypeStruct((nt, rows, 3 * lw), bf16),
            jax.ShapeDtypeStruct((nt, rows, lw), bf16),
            low_b,
            low_b,
            row_b,
        ],
        in_specs=[smem] + whole(10),
        out_specs=whole(7),
        scratch_shapes=[VMEM((rows, width), f32)],
        name="attend",
    )(tix, inputs, gain1, wt_all, tup_all, triple_down, pw_all, pd_all, project_up, gain2, idq)

    mixed_all = gather(mixed, nt, 0)
    sends = pl.pallas_call(
        functools.partial(dispatch_kernel, (nt, capq)),
        out_shape=jax.ShapeDtypeStruct((ne, block, width), bf16),
        in_specs=whole(8),
        out_specs=pl.BlockSpec(memory_space=VMEM),
        scratch_shapes=[VMEM((nt, TOP, rows, 1), f32)],
        name="dispatch",
    )(mixed_all, rt, idc, slotc, slotr, router_weight, router_down, router_up)
    got = swap(sends, ne, 1)

    erows = ne * cp
    quarter = width // nt
    grows = 2 * ffq + quarter + (ADAPT // nt) * (width // 128)
    rets, egrads = pl.pallas_call(
        functools.partial(expert_kernel, (nt, local, capq, cp)),
        out_shape=[
            jax.ShapeDtypeStruct((ne, 2, block, width), bf16),
            jax.ShapeDtypeStruct((nt, grows, 128), bf16),
        ],
        in_specs=whole(8),
        out_specs=whole(2),
        scratch_shapes=[
            VMEM((erows, width), bf16),
            VMEM((erows, width), bf16),
            VMEM((nt, erows, ffq), bf16),
            VMEM((nt, erows, ffq), f32),
            VMEM((2, erows, ADAPT), bf16),
            VMEM((ne, block), f32),
            VMEM((ADAPT, width), f32),
            VMEM((nt, ADAPT, ffq), f32),
            VMEM((nt, ADAPT, ffq), f32),
            VMEM((ADAPT, width), f32),
        ],
        name="experts",
    )(got, got_cot, w1_all, w2_all, first_down, fup_all, sdn_all, second_up)
    back = swap(rets, ne, 2)

    part = jax.ShapeDtypeStruct((nt, rows, width), bf16)
    res_part, grad_part, gg_part = pl.pallas_call(
        functools.partial(combine_kernel, (nt, capq)),
        out_shape=[part, part, jax.ShapeDtypeStruct((nt, TOP, rows), f32)],
        in_specs=whole(3),
        out_specs=whole(3),
        scratch_shapes=[VMEM((ne * block, 1), f32), VMEM((2, ne * block, width), bf16)],
        name="combine",
    )(back, slotc, slotr)
    gmix, res_sum, gg = scatter_sums(grad_part, res_part, gg_part, nt, 3)

    arows = 4 * lw + 2 * quarter + (ADAPT // nt) * (width // 128) + ADAPT // nt
    igrad, agrads = pl.pallas_call(
        functools.partial(back_kernel, (nt, seq, seqp, images)),
        out_shape=[row_b, jax.ShapeDtypeStruct((nt, arows, 128), bf16)],
        in_specs=[smem] + whole(24),
        out_specs=whole(2),
        scratch_shapes=[
            VMEM((2, rows, width), f32),
            VMEM((rows, 3 * lw), bf16),
            VMEM((nt, rows, lw), bf16),
            VMEM((rows, width), f32),
            VMEM((rows, ADAPT), f32),
        ],
        name="attend_back",
    )(
        tix, cotangent, gmix, gg, mixed, middle, triple, attended, tlow, plow, attn_in, inputs,
        gain1, gain2, wt_all, tup_all, triple_down, pw_all, pd_all, project_up, router_weight,
        router_down, router_up, rtq, idq,
    )

    out_q = (middle + res_sum).astype(bf16)
    outs = gather(jnp.stack([out_q, igrad]), nt, 4)

    def unpad(x):
        return x.reshape(images, seqp, width)[:, :seq].reshape(tok, width)

    block_output = unpad(outs[:, 0])
    input_grad = unpad(outs[:, 1])

    held = 2 * ffq
    held_a = 4 * lw
    need = grows + arows
    padded = up(need, 16 * ne)
    rep = up(need - held - held_a, 16)
    parts = [egrads[:, :held], agrads[:, :held_a], egrads[:, held:], agrads[:, held_a:]]
    if padded > need:
        parts.append(jnp.zeros((nt, padded - need, 128), bf16))
    total, shared = reduce_all(jnp.concatenate(parts, axis=1), nt, ne, held + held_a, rep, 5)
    total = total.astype(f32)
    shared = shared.astype(f32)

    def widen(x, n):
        return x.reshape(n, -1, 128).swapaxes(0, 1).reshape(-1, n * 128)

    first_up_grad = widen(total[:ffq], ffq // 128)
    second_down_grad = total[ffq : 2 * ffq]
    triple_up_grad = widen(total[held : held + 3 * lw], 3 * lw // 128).reshape(ADAPT, 3, lw)
    project_down_grad = total[held + 3 * lw : held + 4 * lw]
    share = ADAPT // nt
    cut = [quarter, share * (width // 128), quarter, quarter, share * (width // 128), share]
    pieces, off = [], 0
    for size in cut:
        pieces.append(shared[:, off : off + size])
        off += size

    def wide_all(x):
        return x.reshape(nt, width // 128, share, 128).transpose(0, 2, 1, 3).reshape(ADAPT, width)

    first_down_grad = pieces[0].reshape(width, 128)
    second_up_grad = wide_all(pieces[1])
    triple_down_grad = pieces[2].reshape(width, 128)
    router_down_grad = pieces[3].reshape(width, 128)
    project_up_grad = wide_all(pieces[4])
    router_up_grad = pieces[5].reshape(ADAPT, 128)[:, :experts]
    return (
        block_output, input_grad, triple_down_grad, triple_up_grad, project_down_grad,
        project_up_grad, router_down_grad, router_up_grad, first_down_grad, first_up_grad,
        second_down_grad, second_up_grad,
    )


def solution(mesh):
    return jax.shard_map(
        body,
        mesh=mesh,
        in_specs=(
            P("expert", None),
            P(),
            P(None, None, "tensor"),
            P("tensor", None),
            P(),
            P(),
            P("expert", None, "tensor"),
            P("expert", "tensor", None),
            P(),
            P(None, None, "tensor"),
            P("tensor", None),
            P(),
            P(),
            P(),
            P(),
            P(None, "tensor"),
            P("tensor", None),
            P(),
            P("expert"),
            P("expert", None),
            P("expert", None),
            P("expert", None),
        ),
        out_specs=(
            P("expert", None),
            P("expert", None),
            P(),
            P(None, None, "tensor"),
            P("tensor", None),
            P(),
            P(),
            P(),
            P(),
            P(None, "tensor"),
            P("tensor", None),
            P(),
        ),
        check_vma=False,
    )
```

time: 1140 us -> 423 us (0.37)
  waiting for transfers between devices: 546 us -> 6.29 us
  Pallas kernels: 0 us -> 320 us
  local copies, waits for them, and re-layouts: 219 us -> 64.4 us
  blocking collectives: 108 us -> 0 us
  other arithmetic: 114 us -> 8.68 us
  matrix products: 102 us -> 0 us
  between operations: 15.9 us -> 1.42 us
    psum x5 -> x0, waiting for transfers between devices: 385 us -> none  [the longest x1 150 us: from_experts(): summed = lax.psum(partial_value.astype(jnp.bfloat16), 'tensor')]
    pallas_call x0 -> x12, Pallas kernels: none -> 320 us  [the longest x2 80.7 us: swap(): pl.pallas_call(functools.partial(swap_kernel, n), out_shape=jax.ShapeDtyp...]
    all_to_all x4 -> x1, waiting for transfers between devices: 161 us -> 0.01 us  [body(): got_cot = lax.all_to_all(cots, 'expert', 0, 0, tiled=True)]
    dot_general x46 -> x0, matrix products: 102 us -> none  [the longest x1 8.18 us: body(): jnp.einsum('necr,fr->necf', res_low, second_down, preferred_element_type=...]
    all_to_all x1 -> x0, blocking collectives: 93.9 us -> none  [from_experts(): lax.all_to_all(summed, 'expert', split_axis=0, concat_axis=0, tiled=True)]
    gather x7 -> x1, local copies, waits for them, and re-layouts: 76.9 us -> 0.61 us  [body(): ids = jnp.repeat(adapter_index, seqp, total_repeat_length=images * seqp)]
    reduce_sum x14 -> x0, other arithmetic: 70.1 us -> none  [the longest x1 35.1 us: body(): jnp.sum(back_flat[slot_pairs].astype(f32) * keep_float[:, :, None], axis=1)]
    scatter x6 -> x0, local copies, waits for them, and re-layouts: 67.2 us -> none  [the longest x2 17.8 us: place_pairs(): jnp.zeros((count,), jnp.int32).at[ranking]]
  transfers between devices with their start and end apart: 9 -> 16, of which waited for: 7 -> 2; matrix products, arithmetic and copies ran while one was open for 19% -> 11% of each run, Pallas kernels for 0% -> 23%
where the time goes in v1:
time: 423 us; the launch traced here: 416 us
  Pallas kernels  320 us (76%)
  local copies, waits for them, and re-layouts  64.4 us (15%)
  starting transfers between devices  15.6 us (4%)
  other arithmetic  8.68 us (2%)
  waiting for transfers between devices  6.29 us (1%)
    pallas_call x2, Pallas kernels, swap(): pl.pallas_call(functools.partial(swap_kernel, n), out_shape=jax.ShapeDtyp...  80.7 us
    pallas_call x2, Pallas kernels, gather(): pl.pallas_call(functools.partial(gather_kernel, nt), out_shape=jax.ShapeD...  60.5 us
    pallas_call x1, Pallas kernels, reduce_all(): pl.pallas_call(functools.partial(reduce_kernel, nt, ne, first_rows, rep),...  59.1 us
    pallas_call x1, Pallas kernels, body(): pl.pallas_call(functools.partial(expert_kernel, (nt, local, capq, cp)), o...  32.2 us
    pallas_call x1, Pallas kernels, scatter_sums(): pl.pallas_call(functools.partial(scatter_kernel, nt), out_shape=[jax.Shap...  26.7 us
    dynamic_update_slice x18, local copies, waits for them, and re-layouts, gather_early(): lax.dynamic_update_index_in_dim(out, part, jnp.bitwise_xor(t, mask), 0)  20.2 us
    pallas_call x1, Pallas kernels, body(): pl.pallas_call(functools.partial(back_kernel, (nt, seq, seqp, images)), o...  18.8 us
    unnamed x64, local copies, waits for them, and re-layouts  12.1 us
  transfers between devices with their start and end apart: 16, of which 2 were waited for; matrix products, arithmetic and copies ran while one was open for 11% of the time, Pallas kernels for 23%

profile of v1, /device:TPU:31, one launch (start us, length us, event | category | flops | bytes accessed | tf_op | source)
XLA Modules:
  0.0 416.1 jit_solution(3121179226733151007)
XLA Ops:
  8.6 5.2 %fusion.1 = (f32[1664]{0:T(1024)S(1)}, s32[1664]{0:T(1024)S(1)}) fusion(pred[1664]{0:T(1024)(128)(4,1)S(1)} %copy-done.20, pred[1664]{0:T(1024)(128)(4,1)S(1)} %copy-done.21, pred[1664]{0:T(1024)(128)(4,1)S(1)} %copy-done.22, pred[1664]{0:T(1024)(128)(4,1)S(1)} %copy-done.23, pred[1664]{0:T(1024)(128)(4,1)S(1)} %copy-done.24, ...), kind=kLoop, calls=%fused_computation.42 | loop fusion | flops 13312 | bytes 24992 | tf_op jit(solution)/shard_map/convert_element_type | solution.py:804
  15.4 11.9 %place.1 = (s32[4,416,2]{2,1,0:T(8,128)}, s32[4,2,416]{2,1,0:T(2,128)}, bf16[8,128,512]{2,1,0:T(8,128)(2,1)}) custom-call(s32[1]{0:T(128)} %bitcast.tix, s32[1,1576]{1,0:T(1,128)} %multiply_add_fusion.prio, s32[1664,2]{1,0:T(8,128)} %bitcast.115, f32[4,1,416]{2,1,0:T(1,128)} %convert_element_type.23.idq, bf16[1576,512]{1,0:T(8,128)(2,1)} %cot_ref.1), custom_call_target="tpu_custom_call" | custom-call | tf_op jit(solution)/shard_map/place/pallas_call | solution.py:787
  27.3 5.7 %all-to-all-start = ((bf16[8,128,512]{2,1,0:T(8,128)(2,1)}), bf16[8,128,512]{2,1,0:T(8,128)(2,1)S(1)}, u32[]{:S(2)}, u32[]{:S(2)}) async-start(bf16[8,128,512]{2,1,0:T(8,128)(2,1)} %get-tuple-element.50), calls=%async_computation | async-start | bytes 2097152 | tf_op jit(solution)/shard_map/all_to_all | solution.py:805
  34.2 2.4 broadcast.153.clone
  36.6 2.3 bitcast_dynamic-update-slice_fusion.7
  39.8 2.4 broadcast.153.clone.1
  42.2 2.3 bitcast_dynamic-update-slice_fusion.3
  44.5 1.6 constant_dynamic-slice_fusion.rt
  53.0 1.4 collective-permute-start.7
  54.4 5.0 %collective-permute-done.13 = bf16[2,512,128]{2,1,0:T(8,128)(2,1)S(1)} collective-permute-done((bf16[2,512,128]{2,1,0:T(8,128)(2,1)S(1)}, bf16[2,512,128]{2,1,0:T(8,128)(2,1)S(1)}, u32[]{:S(2)}, u32[]{:S(2)}) %collective-permute-start.13) | collective-permute-done | bytes 262176 | tf_op jit(solution)/shard_map/ppermute | solution.py:593
  59.5 1.9 collective-permute-start.5
  71.9 11.0 %attend.1 = (bf16[416,512]{1,0:T(8,128)(2,1)}, f32[416,512]{1,0:T(8,128)}, bf16[4,416,384]{2,1,0:T(8,128)(2,1)}, bf16[4,416,128]{2,1,0:T(8,128)(2,1)}, bf16[416,...) custom-call(s32[1]{0:T(128)} %bitcast.tix, bf16[1576,512]{1,0:T(8,128)(2,1)} %x_ref.3, ...), custom_call_target="tpu_custom_call" | custom-call | tf_op jit(solution)/shard_map/attend/pallas_call | solution.py:810
  82.8 34.4 %shard_map.301.mixed = bf16[4,416,512]{2,1,0:T(8,128)(2,1)} custom-call(bf16[416,512]{1,0:T(8,128)(2,1)} %get-tuple-element.47.x_ref.mixed), custom_call_target="tpu_custom_call" | custom-call | tf_op jit(solution)/shard_map/pallas_call | solution.py:576
  117.2 9.6 %dispatch.1.x_ref = bf16[8,128,512]{2,1,0:T(8,128)(2,1)} custom-call(bf16[4,416,512]{2,1,0:T(8,128)(2,1)} %shard_map.301.mixed, s32[1664,2]{1,0:T(8,128)} %bitcast.117, s32[1664,1]{1,0:T(8,128)} %select_n.93.idc, s32[4,416,2]{2,1,0:T(8,128)} %get-tuple-element.48.slotc, s32[4,2,416]{2,1,0:T(2,128)} %get-tuple-element.49.slotr, bf16[512,16]{1,0:T(8,128)(2,1)} %copy.57.rw, ...), custom_call_target="tpu_custom_call" | custom-call | tf_op jit(solution)/shard_map/dispatch/pallas_call | solution.py:828
  126.8 28.8 %shard_map.302.got = bf16[8,128,512]{2,1,0:T(8,128)(2,1)} custom-call(bf16[8,128,512]{2,1,0:T(8,128)(2,1)} %dispatch.1.x_ref), custom_call_target="tpu_custom_call" | custom-call | tf_op jit(solution)/shard_map/pallas_call | solution.py:540
  156.7 2.3 bitcast_dynamic-update-slice_fusion.6
  159.1 2.3 bitcast_dynamic-update-slice_fusion.5
  161.3 2.3 bitcast_dynamic-update-slice_fusion.2
  163.7 2.3 bitcast_dynamic-update-slice_fusion.1
  169.0 32.2 %experts.1 = (bf16[8,2,128,512]{3,2,1,0:T(8,128)(2,1)}, bf16[4,1280,128]{2,1,0:T(8,128)(2,1)}) custom-call(bf16[8,128,512]{2,1,0:T(8,128)(2,1)} %shard_map.302.got, bf16[8,128,512]{2,1,0:T(8,128)(2,1)} %copy-done.3, bf16[4,2,512,512]{3,2,1,0:T(8,128)(2,1)} %bitcast_dynamic-update-slice_fusion.4.w1, ...), custom_call_target="tpu_custom_call" | custom-call | tf_op jit(solution)/shard_map/experts/pallas_call | solution.py:841
  201.2 51.9 %shard_map.303.got = bf16[8,2,128,512]{3,2,1,0:T(8,128)(2,1)} custom-call(bf16[8,2,128,512]{3,2,1,0:T(8,128)(2,1)} %get-tuple-element.51.x_ref), custom_call_target="tpu_custom_call" | custom-call | tf_op jit(solution)/shard_map/pallas_call | solution.py:540
  253.1 9.2 %combine.1 = (bf16[4,416,512]{2,1,0:T(8,128)(2,1)}, bf16[4,416,512]{2,1,0:T(8,128)(2,1)}, f32[4,2,416]{2,1,0:T(2,128)}) custom-call(bf16[8,2,128,512]{3,2,1,0:T(8,128)(2,1)} %shard_map.303.got, s32[4,416,2]{2,1,0:T(8,128)} %get-tuple-element.48.slotc, s32[4,2,416]{2,1,0:T(2,128)} %get-tuple-element.49.slotr), custom_call_target="tpu_custom_call" | custom-call | tf_op jit(solution)/shard_map/combine/pallas_call | solution.py:866
  263.6 26.7 %shard_map.304 = (f32[416,512]{1,0:T(8,128)}, f32[416,512]{1,0:T(8,128)}, f32[2,416]{1,0:T(2,128)}) custom-call(bf16[4,416,512]{2,1,0:T(8,128)(2,1)} %get-tuple-element.52.grad, bf16[4,416,512]{2,1,0:T(8,128)(2,1)} %get-tuple-element.53.res, f32[4,2,416]{2,1,0:T(2,128)} %get-tuple-element.54.gg), custom_call_target="tpu_custom_call" | custom-call | tf_op jit(solution)/shard_map/pallas_call | solution.py:635
  290.4 18.8 %attend_back.1 = (bf16[416,512]{1,0:T(8,128)(2,1)}, bf16[4,928,128]{2,1,0:T(8,128)(2,1)}) custom-call(s32[1]{0:T(128)} %bitcast.tix, bf16[1576,512]{1,0:T(8,128)(2,1)} %cot_ref.1, f32[416,512]{1,0:T(8,128)} %get-tuple-element.56.gmix, f32[2,416]{1,0:T(2,128)} %get-tuple-element.57.ggate, bf16[416,512]{1,0:T(8,128)(2,1)} %get-tuple-element.47.x_ref.mixed, ...), custom_call_target="tpu_custom_call" | custom-call | tf_op jit(solution)/shard_map/attend_back/pallas_call | solution.py:877
  312.4 1.4 copy-done.2
  313.8 59.1 %shard_map.306 = (bf16[2304,128]{1,0:T(8,128)(2,1)}, bf16[4,672,128]{2,1,0:T(8,128)(2,1)}) custom-call(bf16[4,2304,128]{2,1,0:T(8,128)(2,1)} %copy-done.2), custom_call_target="tpu_custom_call" | custom-call | tf_op jit(solution)/shard_map/pallas_call | solution.py:711
  373.0 1.7 slice.134
  376.1 2.3 fusion.3
  381.1 26.2 %shard_map.305 = bf16[4,2,416,512]{3,2,1,0:T(8,128)(2,1)} custom-call(bf16[2,416,512]{2,1,0:T(8,128)(2,1)} %pad_maximum_fusion.x_ref), custom_call_target="tpu_custom_call" | custom-call | tf_op jit(solution)/shard_map/pallas_call | solution.py:576
  407.3 2.3 fusion.2
  409.8 1.6 reshape.249
  411.6 1.6 reshape.250
  (141 shorter events, 44.5 us)
Async XLA Ops:
  0.6 38.2 %copy-start = (bf16[128,512]{1,0:T(8,128)(2,1)S(1)}, bf16[128,512]{1,0:T(8,128)(2,1)}, u32[]{:S(2)}) copy-start(bf16[128,512]{1,0:T(8,128)(2,1)} %param.39) | copy-start | bytes 393220
  0.7 7.9 %copy-start.20 = (pred[1664]{0:T(1024)(128)(4,1)S(1)}, pred[1664]{0:T(1024)(128)(4,1)}, u32[]{:S(2)}) copy-start(pred[1664]{0:T(1024)(128)(4,1)} %constant.220) | copy-start | bytes 4996
  0.7 7.8 %copy-start.21 = (pred[1664]{0:T(1024)(128)(4,1)S(1)}, pred[1664]{0:T(1024)(128)(4,1)}, u32[]{:S(2)}) copy-start(pred[1664]{0:T(1024)(128)(4,1)} %constant.221) | copy-start | bytes 4996
  0.7 7.8 %copy-start.22 = (pred[1664]{0:T(1024)(128)(4,1)S(1)}, pred[1664]{0:T(1024)(128)(4,1)}, u32[]{:S(2)}) copy-start(pred[1664]{0:T(1024)(128)(4,1)} %constant.222) | copy-start | bytes 4996
  0.7 7.8 %copy-start.23 = (pred[1664]{0:T(1024)(128)(4,1)S(1)}, pred[1664]{0:T(1024)(128)(4,1)}, u32[]{:S(2)}) copy-start(pred[1664]{0:T(1024)(128)(4,1)} %constant.223) | copy-start | bytes 4996
  0.7 7.8 %copy-start.24 = (pred[1664]{0:T(1024)(128)(4,1)S(1)}, pred[1664]{0:T(1024)(128)(4,1)}, u32[]{:S(2)}) copy-start(pred[1664]{0:T(1024)(128)(4,1)} %constant.224) | copy-start | bytes 4996
  0.7 7.8 %copy-start.25 = (pred[1664]{0:T(1024)(128)(4,1)S(1)}, pred[1664]{0:T(1024)(128)(4,1)}, u32[]{:S(2)}) copy-start(pred[1664]{0:T(1024)(128)(4,1)} %constant.225) | copy-start | bytes 4996
  0.7 7.8 %copy-start.26 = (pred[1664]{0:T(1024)(128)(4,1)S(1)}, pred[1664]{0:T(1024)(128)(4,1)}, u32[]{:S(2)}) copy-start(pred[1664]{0:T(1024)(128)(4,1)} %constant.226) | copy-start | bytes 4996
  0.8 6.1 %copy-start.15 = (s32[8]{0:T(128)S(1)}, s32[8]{0:T(128)}, u32[]{:S(2)}) copy-start(s32[8]{0:T(128)} %param.42) | copy-start | bytes 100
  0.8 6.7 %copy-start.17 = (s32[1576,2]{0,1:T(2,128)S(1)}, s32[1576,2]{0,1:T(2,128)}, u32[]{:S(2)}) copy-start(s32[1576,2]{0,1:T(2,128)} %param.43) | copy-start | bytes 37828
  0.8 7.1 %copy-start.18 = (s32[1,1576]{1,0:T(1,128)S(1)}, s32[1,1576]{1,0:T(1,128)}, u32[]{:S(2)}) copy-start(s32[1,1576]{1,0:T(1,128)} %param.44) | copy-start | bytes 18916
  4.3 60.1 %collective-permute-start = (bf16[640,384]{1,0:T(8,128)(2,1)}, bf16[640,384]{1,0:T(8,128)(2,1)}, u32[]{:S(2)}, u32[]{:S(2)}) collective-permute-start(bf16[640,384]{1,0:T(8,128)(2,1)} %pad_maximum_fusion.1), channel_id=1, source_target_pairs={{0,1},{1,0},{2,3},{3,2},{4,5},{5,4},{6,7},{7,6},{8,9},{9,8},{10,11... | collective-permute-start | bytes 1474568 | tf_op jit(solution)/shard_map/ppermute | solution.py:592
  5.0 60.1 %collective-permute-start.1 = (bf16[640,384]{1,0:T(8,128)(2,1)}, bf16[640,384]{1,0:T(8,128)(2,1)}, u32[]{:S(2)}, u32[]{:S(2)}) collective-permute-start(bf16[640,384]{1,0:T(8,128)(2,1)} %pad_maximum_fusion.1), channel_id=1, source_target_pairs={{0,2},{1,3},{2,0},{3,1},{4,6},{5,7},{6,4},{7,5},{8,10},{9,11},{10,... | collective-permute-start | bytes 1474568 | tf_op jit(solution)/shard_map/ppermute | solution.py:593
  5.3 44.7 %collective-permute-start.3 = (bf16[128,640]{1,0:T(8,128)(2,1)S(1)}, bf16[128,640]{1,0:T(8,128)(2,1)}, u32[]{:S(2)}, u32[]{:S(2)}) collective-permute-start(bf16[128,640]{1,0:T(8,128)(2,1)S(1)} %constant_dynamic-update-slice_fusion), channel_id=1, source_target_pairs={{0,1},{1,0},{2,3},{3,2},{4,5},{5,4},{6,7},{7,6},{8,9},{9,8},{10,11... | collective-permute-start | bytes 491528 | tf_op jit(solution)/shard_map/ppermute | solution.py:592
  5.6 46.2 %collective-permute-start.4 = (bf16[128,640]{1,0:T(8,128)(2,1)S(1)}, bf16[128,640]{1,0:T(8,128)(2,1)}, u32[]{:S(2)}, u32[]{:S(2)}) collective-permute-start(bf16[128,640]{1,0:T(8,128)(2,1)S(1)} %constant_dynamic-update-slice_fusion), channel_id=1, source_target_pairs={{0,2},{1,3},{2,0},{3,1},{4,6},{5,7},{6,4},{7,5},{8,10},{9,11},{10,... | collective-permute-start | bytes 491528 | tf_op jit(solution)/shard_map/ppermute | solution.py:593
  27.3 140.8 %all-to-all-start = ((bf16[8,128,512]{2,1,0:T(8,128)(2,1)}), bf16[8,128,512]{2,1,0:T(8,128)(2,1)S(1)}, u32[]{:S(2)}, u32[]{:S(2)}) async-start(bf16[8,128,512]{2,1,0:T(8,128)(2,1)} %get-tuple-element.50), calls=%async_computation | async-start | bytes 2097152 | tf_op jit(solution)/shard_map/all_to_all | solution.py:805
  33.0 123.8 %collective-permute-start.6 = (bf16[2,512,512]{2,1,0:T(8,128)(2,1)}, bf16[2,512,512]{2,1,0:T(8,128)(2,1)}, u32[]{:S(2)}, u32[]{:S(2)}) collective-permute-start(bf16[2,512,512]{2,1,0:T(8,128)(2,1)} %param.30), channel_id=1, source_target_pairs={{0,1},{1,0},{2,3},{3,2},{4,5},{5,4},{6,7},{7,6},{8,9},{9,8},{10,11... | collective-permute-start | bytes 3145736 | tf_op jit(solution)/shard_map/ppermute | solution.py:592
  42.2 6.0 %copy-start.16 = (bf16[512,16]{0,1:T(8,128)(2,1)S(1)}, bf16[512,16]{0,1:T(8,128)(2,1)}, u32[]{:S(2)}) copy-start(bf16[512,16]{0,1:T(8,128)(2,1)} %param.29) | copy-start | bytes 49156
  42.2 6.8 %copy-start.19 = (bf16[128,16]{0,1:T(8,128)(2,1)S(1)}, bf16[128,16]{0,1:T(8,128)(2,1)}, u32[]{:S(2)}) copy-start(bf16[128,16]{0,1:T(8,128)(2,1)} %param.37) | copy-start | bytes 12292
  50.7 2.3 collective-permute-start.12
  51.8 7.6 %collective-permute-start.13 = (bf16[2,512,128]{2,1,0:T(8,128)(2,1)S(1)}, bf16[2,512,128]{2,1,0:T(8,128)(2,1)S(1)}, u32[]{:S(2)}, u32[]{:S(2)}) collective-permute-start(bf16[2,512,128]{2,1,0:T(8,128)(2,1)S(1)} %copy-done.12), channel_id=1, source_target_pairs={{0,2},{1,3},{2,0},{3,1},{4,6},{5,7},{6,4},{7,5},{8,10},{9,11},{10,... | collective-permute-start | bytes 786440 | tf_op jit(solution)/shard_map/ppermute | solution.py:593
  53.0 102.7 %collective-permute-start.7 = (bf16[2,512,512]{2,1,0:T(8,128)(2,1)}, bf16[2,512,512]{2,1,0:T(8,128)(2,1)}, u32[]{:S(2)}, u32[]{:S(2)}) collective-permute-start(bf16[2,512,512]{2,1,0:T(8,128)(2,1)} %param.30), channel_id=1, source_target_pairs={{0,2},{1,3},{2,0},{3,1},{4,6},{5,7},{6,4},{7,5},{8,10},{9,11},{10,... | collective-permute-start | bytes 3145736 | tf_op jit(solution)/shard_map/ppermute | solution.py:593
  59.5 3.1 collective-permute-start.5
  62.6 94.1 %collective-permute-start.10 = (bf16[2,512,512]{2,1,0:T(8,128)(2,1)}, bf16[2,512,512]{2,1,0:T(8,128)(2,1)}, u32[]{:S(2)}, u32[]{:S(2)}) collective-permute-start(bf16[2,512,512]{2,1,0:T(8,128)(2,1)} %param.31), channel_id=1, source_target_pairs={{0,2},{1,3},{2,0},{3,1},{4,6},{5,7},{6,4},{7,5},{8,10},{9,11},{10,... | collective-permute-start | bytes 3145736 | tf_op jit(solution)/shard_map/ppermute | solution.py:593
  64.4 3.0 collective-permute-start.14
  65.1 4.6 %collective-permute-start.2 = (bf16[640,384]{1,0:T(8,128)(2,1)}, bf16[640,384]{1,0:T(8,128)(2,1)S(1)}, u32[]{:S(2)}, u32[]{:S(2)}) collective-permute-start(bf16[640,384]{1,0:T(8,128)(2,1)} %collective-permute-done.1), channel_id=1, source_target_pairs={{0,1},{1,0},{2,3},{3,2},{4,5},{5,4},{6,7},{7,6},{8,9},{9,8},{10,11... | collective-permute-start | bytes 1474568 | tf_op jit(solution)/shard_map/ppermute | solution.py:594
  67.4 94.0 %collective-permute-start.9 = (bf16[2,512,512]{2,1,0:T(8,128)(2,1)}, bf16[2,512,512]{2,1,0:T(8,128)(2,1)}, u32[]{:S(2)}, u32[]{:S(2)}) collective-permute-start(bf16[2,512,512]{2,1,0:T(8,128)(2,1)} %param.31), channel_id=1, source_target_pairs={{0,1},{1,0},{2,3},{3,2},{4,5},{5,4},{6,7},{7,6},{8,9},{9,8},{10,11... | collective-permute-start | bytes 3145736 | tf_op jit(solution)/shard_map/ppermute | solution.py:592
  155.6 10.3 %collective-permute-start.8 = (bf16[2,512,512]{2,1,0:T(8,128)(2,1)}, bf16[2,512,512]{2,1,0:T(8,128)(2,1)S(1)}, u32[]{:S(2)}, u32[]{:S(2)}) collective-permute-start(bf16[2,512,512]{2,1,0:T(8,128)(2,1)} %collective-permute-done.7), channel_id=1, source_target_pairs={{0,1},{1,0},{2,3},{3,2},{4,5},{5,4},{6,7},{7,6},{8,9},{9,8},{10,11... | collective-permute-start | bytes 3145736 | tf_op jit(solution)/shard_map/ppermute | solution.py:594
  156.7 10.4 %collective-permute-start.11 = (bf16[2,512,512]{2,1,0:T(8,128)(2,1)}, bf16[2,512,512]{2,1,0:T(8,128)(2,1)S(1)}, u32[]{:S(2)}, u32[]{:S(2)}) collective-permute-start(bf16[2,512,512]{2,1,0:T(8,128)(2,1)} %collective-permute-done.10), channel_id=1, source_target_pairs={{0,1},{1,0},{2,3},{3,2},{4,5},{5,4},{6,7},{7,6},{8,9},{9,8},{10,11... | collective-permute-start | bytes 3145736 | tf_op jit(solution)/shard_map/ppermute | solution.py:594
  372.9 6.2 %copy-start.7 = (bf16[2304,128]{1,0:T(8,128)(2,1)S(1)}, bf16[2304,128]{1,0:T(8,128)(2,1)}, u32[]{:S(2)}) copy-start(bf16[2304,128]{1,0:T(8,128)(2,1)} %get-tuple-element.67) | copy-start | bytes 1769476
  372.9 7.0 %copy-start.4 = (f32[416,512]{1,0:T(8,128)S(1)}, f32[416,512]{1,0:T(8,128)}, u32[]{:S(2)}) copy-start(f32[416,512]{1,0:T(8,128)} %get-tuple-element.46.middle) | copy-start | bytes 2555908
  372.9 7.0 %copy-start.9 = (f32[416,512]{1,0:T(8,128)S(1)}, f32[416,512]{1,0:T(8,128)}, u32[]{:S(2)}) copy-start(f32[416,512]{1,0:T(8,128)} %get-tuple-element.55) | copy-start | bytes 2555908
  (11 other events, 31.7 us)
